TPU v7x, 128 devices: a whole 4x4x4 slice. The times are simulated.
128 devices in a mesh: gx: 16 (over z, x), gy: 8 (over y, core).
Axes of the slice: x: 4, y: 4, z: 4, core: 2. Of those that a mesh axis runs over, the one named last changes fastest.
Arguments:
- cotangent: float32 [16, 8, 42, 1024], P('gx', 'gy'), may hold values from -6 to 6
- section_states: bfloat16 [3, 16, 8, 42, 1024], P(None, 'gx', 'gy'), may hold values from -6 to 6
- inverse_area: float32 [16, 8, 1024], P('gx', 'gy'), may hold values from 0.5 to 2
- edge_length: float32 [16, 8, 3, 1024], P('gx', 'gy'), may hold values from 0.5 to 1.5
- roughness: float32 [16, 8, 1024], P('gx', 'gy'), may hold values from 0.5 to 2
- soil_conductance: float32 [16, 8, 1024], P('gx', 'gy'), may hold values from 0.5 to 2
- zone_friction: float32 [512], replicated, may hold values from 0.25 to 1
- zone_conductivity: float32 [512], replicated, may hold values from 0.25 to 1
- wet_mask: int32 [16, 8, 1024], P('gx', 'gy'), may hold values 0 or 1
- element_zone: int32 [16, 8, 1024], P('gx', 'gy'), may hold values from 0 to 511, as said below
- send_face: int32 [16, 8, 8, 256], P('gx', 'gy'), may hold values from 0 to 3071, as said below
- send_count: int32 [16, 8, 8], P('gx', 'gy'), may hold values from 0 to 256, as said below
- face_partner: int32 [16, 8, 3, 1024], P('gx', 'gy'), may hold values from 0 to 4867, as said below
- volume_matrix: float32 [12, 12], replicated, may hold values from -1.75 to 1.75
- flux_in: float32 [8, 8], replicated, may hold values from -2 to 2
- flux_out: float32 [8, 8], replicated, may hold values from -2 to 2
Outputs:
- adjoint: float32 [16, 8, 42, 1024], P('gx', 'gy')
- zone_grads: float32 [2, 512], replicated
Inputs may be any that keep to these rules, and one draw needn't show every extreme that they name: `element_zone`: zones lie near their partition: an element of partition (a, b) has a zone among the 8 zones from (a*8+b)*4 on, modulo 512. send_count[a, b, n] equals send_count of the partition at offset n for offset 7 - n; it is 0 where that partition lies outside the grid, 1 to 4 for the four diagonal offsets (4 for some pair in every draw), at least 192 for the others, and 256 for some pair in every draw. `send_face`: the live slots of a partition name distinct faces; slots at or beyond the count hold 0. `face_partner`: the faces are paired: a face sent in slot j to offset n faces entry 3072 + n*256 + j, the other faces face a local face whose partner they are, or themselves.
All inputs are finite; a program needn't handle non-finite values. No bound on the sum of `wet_mask` on one device may be relied on, other than what follows from the above.
Results may differ from a plain program's by a relative error of at most 0.0003.
Values may be sent and summed in bfloat16 or wider, within the bound.
A program may use at most 64 MiB of HBM per device.

v0:
```python
import jax
import jax.numpy as jnp
import numpy as np
from jax import lax
from jax.sharding import PartitionSpec as P

LAYERS = 10
ZONE_DEV = 4


TIME_STEP = 0.2
SALT_RETURN = 0.5
LATERAL = 0.5
GRAD_WEIGHT = 1.0 / 64.0
FACE_NODES = ((1, 2), (2, 0), (0, 1))
MOMENTUM_ROWS = np.array([0, 0, 0, 1, 1, 1, 1, 1, 1, 0, 0, 0], np.float32)


def shifted(x, axis, by):
    peers = lax.axis_size(axis)
    pairs = [(i, i + by) for i in range(peers) if 0 <= i + by < peers]
    return lax.ppermute(x, axis, pairs)


def trace_rows():
    channels = 8 + 2 * LAYERS
    rows = np.zeros((channels, 3), np.int32)
    for face_no in range(3):
        for end_no in range(2):
            node_no = FACE_NODES[face_no][end_no]
            for comp_no in range(4):
                rows[comp_no * 2 + end_no, face_no] = comp_no * 3 + node_no
            for layer_no in range(LAYERS):
                rows[8 + layer_no * 2 + end_no, face_no] = 12 + layer_no * 3 + node_no
    return rows.reshape(-1)


def take_traces(state, rows):
    channels = rows.shape[0] // 3
    return state[rows].reshape(channels, 3 * state.shape[1])


def lift_back(flux, rows, row_count):
    return jnp.zeros((row_count, flux.shape[-1]), jnp.float32).at[rows].add(flux)


def section_speed(flat_traces, outer_flat):
    return jnp.sqrt(1.0 + 0.25 * jnp.mean(flat_traces[:8] ** 2 + outer_flat[:8] ** 2, axis=0))


def local_operator(
    state,
    received,
    conductivity,
    friction,
    wave_speed,
    inverse_area,
    edge_length,
    wet_mask,
    partner,
    volume_matrix,
    flux_in,
    flux_out,
    rows,
):
    element_count = state.shape[1]
    channels = rows.shape[0] // 3
    flat_traces = take_traces(state, rows)
    trace_table = jnp.concatenate([flat_traces, received.reshape(channels, -1)], axis=1)
    outer_traces = trace_table[:, partner.reshape(-1)].reshape(channels, 3, element_count)
    inner_traces = flat_traces.reshape(channels, 3, element_count)
    surf_inner = inner_traces[:8]
    surf_outer = outer_traces[:8]
    flux_surface = (
        jnp.einsum("ab,bfe->afe", flux_in, surf_inner, precision=lax.Precision.HIGHEST)
        - jnp.einsum("ab,bfe->afe", flux_out, surf_outer, precision=lax.Precision.HIGHEST)
        + 0.5 * wave_speed[None] * (surf_inner - surf_outer)
    )
    flux_pore = LATERAL * conductivity[None, None] * (outer_traces[8:] - inner_traces[8:])
    flux_all = jnp.concatenate([flux_surface, flux_pore], axis=0) * edge_length[None]
    lifted = lift_back(flux_all.reshape(channels * 3, element_count), rows, state.shape[0])
    volume = jnp.dot(volume_matrix, state[:12], precision=lax.Precision.HIGHEST)
    top_exchange = conductivity[None] * (state[9:12] - state[12:15])
    momentum = jnp.asarray(MOMENTUM_ROWS, dtype=jnp.float32)[:, None]
    surface = inverse_area[None] * (volume + lifted[:12]) - momentum * friction[None] * state[:12]
    surface = (
        jnp.concatenate([surface[:9], surface[9:12] - SALT_RETURN * top_exchange], axis=0)
        * wet_mask[None]
    )
    layers = state[12:].reshape(LAYERS, 3, element_count)
    between = conductivity[None, None] * (layers[:-1] - layers[1:])
    from_above = jnp.concatenate([top_exchange[None], between], axis=0)
    to_below = jnp.concatenate([between, jnp.zeros((1, 3, element_count), jnp.float32)], axis=0)
    pore = (from_above - to_below).reshape(3 * LAYERS, element_count) + inverse_area[None] * lifted[
        12:
    ]
    return jnp.concatenate([surface, pore], axis=0)


def forward_estuary(block, by_count):
    return shifted(block, "gx", by_count)


def forward_across(block, by_count):
    return shifted(block, "gy", by_count)


def backward_estuary(block, by_count):
    return shifted(block, "gx", by_count)


def backward_across(block, by_count):
    return shifted(block, "gy", by_count)


def route_blocks(blocks, estuary_hop, across_hop):
    pieces = [
        across_hop(estuary_hop(blocks[..., 7, :], 1), 1),
        estuary_hop(blocks[..., 6, :], 1),
        across_hop(estuary_hop(blocks[..., 5, :], 1), -1),
        across_hop(blocks[..., 4, :], 1),
        across_hop(blocks[..., 3, :], -1),
        across_hop(estuary_hop(blocks[..., 2, :], -1), 1),
        estuary_hop(blocks[..., 1, :], -1),
        across_hop(estuary_hop(blocks[..., 0, :], -1), -1),
    ]
    return jnp.stack(pieces, axis=-2)


def local(
    cotangent,
    section_states,
    inverse_area,
    edge_length,
    roughness,
    soil_conductance,
    zone_friction,
    zone_conductivity,
    wet_mask,
    element_zone,
    send_face,
    send_count,
    face_partner,
    volume_matrix,
    flux_in,
    flux_out,
):
    rows = jnp.asarray(trace_rows(), dtype=jnp.int32)
    channels = rows.shape[0] // 3
    cotangent_local = cotangent[0, 0]
    row_count = cotangent_local.shape[0]
    element_count = cotangent_local.shape[1]
    area_local = inverse_area[0, 0]
    edges_local = edge_length[0, 0]
    rough_local = roughness[0, 0]
    conduct_local = soil_conductance[0, 0]
    wetness = wet_mask[0, 0].astype(jnp.float32)
    zones_local = element_zone[0, 0]
    faces_sent = send_face[0, 0]
    counts_sent = send_count[0, 0]
    partner = face_partner[0, 0]
    zone_total = zone_friction.shape[0]
    conductivity = zone_conductivity[zones_local] * conduct_local
    zone_factor = zone_friction[zones_local]
    slot_index = jnp.arange(faces_sent.shape[1])
    live_slots = (slot_index[None, :] < counts_sent[:, None]).astype(jnp.float32)
    device_number = lax.axis_index("gx") * lax.axis_size("gy") + lax.axis_index("gy")
    zone_base = device_number * ZONE_DEV
    near_count = 2 * ZONE_DEV
    offset_zone = (zones_local - zone_base) % zone_total
    near_onehot = (offset_zone[None, :] == jnp.arange(near_count, dtype=jnp.int32)[:, None]).astype(
        jnp.float32
    )
    near_ids = (zone_base + jnp.arange(near_count, dtype=jnp.int32)) % zone_total
    forward_all = section_states[:, 0, 0].astype(jnp.float32)

    def section_received(states):
        flat_states = jax.vmap(lambda one: take_traces(one, rows))(states)
        outgoing = (flat_states[:, :, faces_sent] * live_slots[None, None]).astype(jnp.bfloat16)
        return route_blocks(outgoing, forward_estuary, forward_across).astype(jnp.float32)

    def received_of(section_no):
        return section_received(forward_all[section_no : section_no + 1])[0]

    def section_adjoint(section_no, weight_field):
        forward_state = forward_all[section_no]
        flat_forward = take_traces(forward_state, rows)
        received = received_of(section_no)
        trace_table = jnp.concatenate([flat_forward, received.reshape(channels, -1)], axis=1)
        outer_forward = trace_table[:, partner.reshape(-1)]
        wave_speed = section_speed(flat_forward, outer_forward).reshape(3, element_count)
        moment = jnp.sqrt(1.0 + jnp.mean(forward_state[3:9] ** 2, axis=0))
        friction_base = rough_local * moment
        friction = zone_factor * friction_base

        def section_operator(state, incoming, conduct_in, friction_in):
            return local_operator(
                state,
                incoming,
                conduct_in,
                friction_in,
                wave_speed,
                area_local,
                edges_local,
                wetness,
                partner,
                volume_matrix,
                flux_in,
                flux_out,
                rows,
            )

        unused, pullback = jax.vjp(
            section_operator, forward_state, received, conductivity, friction
        )
        state_bar, received_bar, conduct_bar, friction_bar = pullback(TIME_STEP * weight_field)
        returned = route_blocks(received_bar, backward_estuary, backward_across)
        flat_bar = (
            jnp.zeros((channels, 3 * element_count), jnp.float32)
            .at[:, faces_sent]
            .add(returned * live_slots[None])
        )
        state_bar = state_bar + lift_back(
            flat_bar.reshape(channels * 3, element_count), rows, row_count
        )
        element_terms = jnp.stack(
            [friction_base * friction_bar, conduct_local * conduct_bar], axis=0
        )
        near_terms = jnp.einsum(
            "ke,ze->kz", element_terms, near_onehot, precision=lax.Precision.HIGHEST
        )
        zone_terms = jnp.zeros((2, zone_total), jnp.float32).at[:, near_ids].add(near_terms)
        return (state_bar, zone_terms)

    bar_two, terms_two = section_adjoint(2, cotangent_local)
    lam_two = 2.0 / 3.0 * (cotangent_local + bar_two)
    bar_one, terms_one = section_adjoint(1, lam_two)
    lam_one = 0.25 * (lam_two + bar_one)
    bar_zero, terms_zero = section_adjoint(0, lam_one)
    adjoint = cotangent_local / 3.0 + 0.75 * lam_two + lam_one + bar_zero
    summed = [lax.psum(terms, ("gx", "gy")) for terms in (terms_two, terms_one, terms_zero)]
    zone_grads = GRAD_WEIGHT * (2.0 / 3.0 * summed[0] + 0.25 * summed[1] + summed[2])
    return (adjoint[None, None], zone_grads)


def solution(mesh):
    placed = (
        P("gx", "gy", None, None),
        P(None, "gx", "gy", None, None),
        P("gx", "gy", None),
        P("gx", "gy", None, None),
        P("gx", "gy", None),
        P("gx", "gy", None),
        P(),
        P(),
        P("gx", "gy", None),
        P("gx", "gy", None),
        P("gx", "gy", None, None),
        P("gx", "gy", None),
        P("gx", "gy", None, None),
        P(),
        P(),
        P(),
    )
    return jax.shard_map(
        local,
        mesh=mesh,
        in_specs=placed,
        out_specs=(P("gx", "gy", None, None), P()),
        check_vma=False,
    )
```

profile of v0, /device:TPU:33, one launch (start us, length us, event | category | flops | bytes accessed | tf_op | source)
XLA Modules:
  0.0 641.7 jit_solution(15260128408146421137)
XLA Ops:
  5.4 7.6 %gather_fusion.12 = f32[2048,28]{1,0:T(8,128)} fusion(f32[28,3072]{0,1:T(8,128)S(1)} %copy.369, s32[2048]{0:T(1024)S(1)} %broadcast_clamp_fusion.1), kind=kCustom, calls=%fused_computation.15 | custom fusion | bytes 466944 | tf_op jit(solution)/shard_map/gather | solution.py:179
  13.0 2.3 copy.370
  17.5 7.6 %gather_fusion.8 = f32[2048,28]{1,0:T(8,128)} fusion(f32[28,3072]{0,1:T(8,128)S(1)} %copy.340, s32[2048]{0:T(1024)S(1)} %broadcast_clamp_fusion.1), kind=kCustom, calls=%fused_computation.10 | custom fusion | bytes 466944 | tf_op jit(solution)/shard_map/gather | solution.py:179
  25.1 2.3 copy.341
  29.0 7.6 %gather_fusion.4 = f32[2048,28]{1,0:T(8,128)} fusion(f32[28,3072]{0,1:T(8,128)S(1)} %copy.311, s32[2048]{0:T(1024)S(1)} %broadcast_clamp_fusion.1), kind=kCustom, calls=%fused_computation.5 | custom fusion | bytes 466944 | tf_op jit(solution)/shard_map/gather | solution.py:179
  40.8 3.1 collective-permute-start
  43.9 3.1 collective-permute-start.2
  47.0 2.8 collective-permute-start.3
  49.9 4.6 collective-permute-start.5
  59.3 6.9 %gather_fusion = f32[1024]{0:T(1024)S(1)} fusion(f32[512]{0:T(512)S(1)} %copy-done.1, s32[1024]{0:T(1024)S(1)} %broadcast_clamp_fusion.2), kind=kCustom, calls=%fused_computation | custom fusion | bytes 12288 | tf_op jit(solution)/shard_map/gather | solution.py:163
  66.2 6.9 %gather_fusion.1 = f32[1024]{0:T(1024)S(1)} fusion(f32[512]{0:T(512)S(1)} %copy-done.2, s32[1024]{0:T(1024)S(1)} %broadcast_clamp_fusion.2), kind=kCustom, calls=%fused_computation.1 | custom fusion | bytes 12288 | tf_op jit(solution)/shard_map/gather | solution.py:164
  82.1 4.6 collective-permute-start.7
  86.7 2.2 collective-permute-start.9
  89.4 2.2 collective-permute-start.10
  91.6 3.1 collective-permute-start.26
  94.7 4.8 collective-permute-start.29
  101.5 4.3 collective-permute-start.33
  107.7 3.9 collective-permute-start.53
  113.6 5.8 collective-permute-start.57
  119.4 3.9 collective-permute-start.1
  129.8 3.6 collective-permute-start.8
  150.4 5.5 collective-permute-start.31
  156.6 3.4 collective-permute-start.34
  162.7 4.5 collective-permute-start.25
  167.2 2.1 collective-permute-start.28
  172.6 10.9 %gather_fusion.5 = f32[3072,28]{1,0:T(8,128)} fusion(f32[28,5120]{0,1:T(8,128)S(1)} %copy.321, s32[3072]{0:T(1024)S(1)} %copy-done.60), kind=kCustom, calls=%fused_computation.6 | custom fusion | bytes 700416 | tf_op jit(solution)/shard_map/gather | solution.py:190
  190.1 17.9 %scatter_custom_fusion = f32[28,5120]{0,1:T(8,128)S(1)} fusion(s32[3072]{0:T(1024)} %bitcast.397, f32[3072,28]{1,0:T(8,128)} %copy.327, f32[]{:T(128)} %constant.38.clone.1), kind=kCustom, calls=%fused_computation.36 | custom fusion | flops 86016 | bytes 573952 | tf_op jit(solution)/shard_map/transpose(jvp())/scatter-add | solution.py:70
  211.8 5.5 collective-permute-start.55
  217.3 3.4 collective-permute-start.58
  220.7 4.5 collective-permute-start.32
  232.1 3.6 collective-permute-start.49
  237.7 3.6 collective-permute-start.56
  249.4 11.9 %gather_fusion.9 = f32[3072,28]{1,0:T(8,128)} fusion(f32[28,5120]{0,1:T(8,128)S(1)} %copy.350, s32[3072]{0:T(1024)} %broadcast_clamp_fusion), kind=kCustom, calls=%fused_computation.11 | custom fusion | bytes 700416 | tf_op jit(solution)/shard_map/gather | solution.py:190
  269.5 2.9 collective-permute-start.15
  273.2 4.5 collective-permute-start.17
  284.4 11.9 %gather_fusion.13 = f32[3072,28]{1,0:T(8,128)} fusion(f32[28,5120]{0,1:T(8,128)S(1)} %copy.379, s32[3072]{0:T(1024)} %broadcast_clamp_fusion), kind=kCustom, calls=%fused_computation.16 | custom fusion | bytes 700416 | tf_op jit(solution)/shard_map/gather | solution.py:190
  298.6 4.2 collective-permute-start.19
  302.8 3.6 collective-permute-start.22
  307.2 3.3 collective-permute-start.21
  310.5 4.5 collective-permute-start.13
  317.0 3.6 collective-permute-start.20
  320.6 2.1 collective-permute-start.23
  336.6 13.9 %scatter_custom_fusion.2 = f32[28,3072]{0,1:T(8,128)S(1)} fusion(s32[2048]{0:T(1024)} %bitcast.407, f32[2048,28]{1,0:T(8,128)} %bitcast.370, f32[]{:T(128)} %constant.38.clone.1), kind=kCustom, calls=%fused_computation.57 | custom fusion | flops 57344 | bytes 344576 | tf_op jit(solution)/shard_map/scatter-add | solution.py:221
  363.2 17.9 %scatter_custom_fusion.4 = f32[28,5120]{0,1:T(8,128)S(1)} fusion(s32[3072]{0:T(1024)} %bitcast.398, f32[3072,28]{1,0:T(8,128)} %copy.356, f32[]{:T(128)} %constant.38.clone.1), kind=kCustom, calls=%fused_computation.34 | custom fusion | flops 86016 | bytes 573952 | tf_op jit(solution)/shard_map/transpose(jvp())/scatter-add | solution.py:70
  390.9 3.0 collective-permute-start.39
  395.5 4.4 collective-permute-start.41
  402.9 2.3 fusion.116
  410.2 4.1 collective-permute-start.43
  414.3 4.0 collective-permute-start.46
  420.8 3.3 collective-permute-start.45
  424.1 4.5 collective-permute-start.37
  430.6 3.6 collective-permute-start.44
  448.7 13.7 %scatter_custom_fusion.6 = f32[28,3072]{0,1:T(8,128)S(1)} fusion(s32[2048]{0:T(1024)} %bitcast.408, f32[2048,28]{1,0:T(8,128)S(1)} %bitcast.371, f32[]{:T(128)} %constant.38.clone.1), kind=kCustom, calls=%fused_computation.55 | custom fusion | flops 57344 | bytes 344576 | tf_op jit(solution)/shard_map/scatter-add | solution.py:221
  474.9 17.9 %scatter_custom_fusion.8 = f32[28,5120]{0,1:T(8,128)S(1)} fusion(s32[3072]{0:T(1024)} %bitcast.399, f32[3072,28]{1,0:T(8,128)} %copy.385, f32[]{:T(128)} %constant.38.clone.1), kind=kCustom, calls=%fused_computation.32 | custom fusion | flops 86016 | bytes 573952 | tf_op jit(solution)/shard_map/transpose(jvp())/scatter-add | solution.py:70
  502.6 3.2 collective-permute-start.63
  506.5 4.4 collective-permute-start.65
  511.0 2.1 collective-permute-start.66
  518.4 70.7 %all-reduce.42 = (f32[2,512]{0,1:T(8,128)}, f32[2,512]{0,1:T(8,128)}, f32[2,512]{0,1:T(8,128)}) all-reduce(f32[2,512]{0,1:T(8,128)S(1)} %scatter_custom_fusion.14, f32[2,512]{0,1:T(8,128)S(1)} %scatter_custom_fusion.13, f32[2,512]{0,1:T(8,128)} %scatter_custom_fusion.12), channel_id=1, replica_groups=mesh['gx'=16,'gy'=8] {'gx','gy'}, use_global_device_ids=true, to_apply=%region_35.36 | all-reduce | flops 3072 | bytes 24576 | tf_op jit(solution)/shard_map/psum | solution.py:241
  594.4 4.1 collective-permute-start.67
  598.5 2.4 collective-permute-start.70
  603.4 2.4 collective-permute-start.69
  607.8 2.3 collective-permute-start.64
  610.2 3.2 collective-permute-start.68
  624.9 13.7 %scatter_custom_fusion.10 = f32[28,3072]{0,1:T(8,128)S(1)} fusion(s32[2048]{0:T(1024)} %bitcast.409, f32[2048,28]{1,0:T(8,128)S(1)} %bitcast.369, f32[]{:T(128)} %constant.38.clone.1), kind=kCustom, calls=%fused_computation.53 | custom fusion | flops 57344 | bytes 344576 | tf_op jit(solution)/shard_map/scatter-add | solution.py:221
  (692 shorter events, 225.1 us)
Async XLA Ops:
  40.8 41.3 %collective-permute-start = (bf16[1,28,256]{2,1,0:T(8,128)(2,1)}, bf16[1,28,256]{2,1,0:T(8,128)(2,1)}, u32[]{:S(2)}, u32[]{:S(2)}) collective-permute-start(bf16[1,28,256]{2,1,0:T(8,128)(2,1)} %get-tuple-element.115), channel_id=1, source_target_pairs={{0,8},{8,16},{16,24},{24,32},{32,40},{40,48},{48,56},{56,64},{64,7... | collective-permute-start | bytes 43016 | tf_op jit(solution)/shard_map/ppermute | solution.py:22
  43.9 42.7 %collective-permute-start.2 = (bf16[1,28,256]{2,1,0:T(8,128)(2,1)}, bf16[1,28,256]{2,1,0:T(8,128)(2,1)}, u32[]{:S(2)}, u32[]{:S(2)}) collective-permute-start(bf16[1,28,256]{2,1,0:T(8,128)(2,1)} %get-tuple-element.114), channel_id=1, source_target_pairs={{0,8},{8,16},{16,24},{24,32},{32,40},{40,48},{48,56},{56,64},{64,7... | collective-permute-start | bytes 43016 | tf_op jit(solution)/shard_map/ppermute | solution.py:22
  47.0 42.4 %collective-permute-start.3 = (bf16[1,28,256]{2,1,0:T(8,128)(2,1)}, bf16[1,28,256]{2,1,0:T(8,128)(2,1)}, u32[]{:S(2)}, u32[]{:S(2)}) collective-permute-start(bf16[1,28,256]{2,1,0:T(8,128)(2,1)} %get-tuple-element.113), channel_id=1, source_target_pairs={{0,8},{8,16},{16,24},{24,32},{32,40},{40,48},{48,56},{56,64},{64,7... | collective-permute-start | bytes 43016 | tf_op jit(solution)/shard_map/ppermute | solution.py:22
  49.9 41.7 %collective-permute-start.5 = (bf16[1,28,256]{2,1,0:T(8,128)(2,1)}, bf16[1,28,256]{2,1,0:T(8,128)(2,1)}, u32[]{:S(2)}, u32[]{:S(2)}) collective-permute-start(bf16[1,28,256]{2,1,0:T(8,128)(2,1)} %get-tuple-element.112), channel_id=1, source_target_pairs={{0,1},{1,2},{2,3},{3,4},{4,5},{5,6},{6,7},{8,9},{9,10},{10,11},{11... | collective-permute-start | bytes 43016 | tf_op jit(solution)/shard_map/ppermute | solution.py:22
  54.5 40.3 %collective-permute-start.6 = (bf16[1,28,256]{2,1,0:T(8,128)(2,1)}, bf16[1,28,256]{2,1,0:T(8,128)(2,1)}, u32[]{:S(2)}, u32[]{:S(2)}) collective-permute-start(bf16[1,28,256]{2,1,0:T(8,128)(2,1)} %get-tuple-element.111), channel_id=1, source_target_pairs={{1,0},{2,1},{3,2},{4,3},{5,4},{6,5},{7,6},{9,8},{10,9},{11,10},{12... | collective-permute-start | bytes 43016 | tf_op jit(solution)/shard_map/ppermute | solution.py:22
  82.1 17.4 %collective-permute-start.7 = (bf16[1,28,256]{2,1,0:T(8,128)(2,1)S(1)}, bf16[1,28,256]{2,1,0:T(8,128)(2,1)}, u32[]{:S(2)}, u32[]{:S(2)}) collective-permute-start(bf16[1,28,256]{2,1,0:T(8,128)(2,1)S(1)} %copy-done.105), channel_id=1, source_target_pairs={{8,0},{16,8},{24,16},{32,24},{40,32},{48,40},{56,48},{64,56},{72,6... | collective-permute-start | bytes 43016 | tf_op jit(solution)/shard_map/ppermute | solution.py:22
  89.4 16.3 %collective-permute-start.10 = (bf16[1,28,256]{2,1,0:T(8,128)(2,1)S(1)}, bf16[1,28,256]{2,1,0:T(8,128)(2,1)}, u32[]{:S(2)}, u32[]{:S(2)}) collective-permute-start(bf16[1,28,256]{2,1,0:T(8,128)(2,1)S(1)} %copy-done.103), channel_id=1, source_target_pairs={{8,0},{16,8},{24,16},{32,24},{40,32},{48,40},{56,48},{64,56},{72,6... | collective-permute-start | bytes 43016 | tf_op jit(solution)/shard_map/ppermute | solution.py:22
  91.6 16.1 %collective-permute-start.26 = (bf16[1,28,256]{2,1,0:T(8,128)(2,1)}, bf16[1,28,256]{2,1,0:T(8,128)(2,1)S(1)}, u32[]{:S(2)}, u32[]{:S(2)}) collective-permute-start(bf16[1,28,256]{2,1,0:T(8,128)(2,1)} %get-tuple-element.106), channel_id=1, source_target_pairs={{0,8},{8,16},{16,24},{24,32},{32,40},{40,48},{48,56},{56,64},{64,7... | collective-permute-start | bytes 43016 | tf_op jit(solution)/shard_map/ppermute | solution.py:22
  94.7 16.9 %collective-permute-start.29 = (bf16[1,28,256]{2,1,0:T(8,128)(2,1)}, bf16[1,28,256]{2,1,0:T(8,128)(2,1)S(1)}, u32[]{:S(2)}, u32[]{:S(2)}) collective-permute-start(bf16[1,28,256]{2,1,0:T(8,128)(2,1)} %get-tuple-element.104), channel_id=1, source_target_pairs={{0,1},{1,2},{2,3},{3,4},{4,5},{5,6},{6,7},{8,9},{9,10},{10,11},{11... | collective-permute-start | bytes 43016 | tf_op jit(solution)/shard_map/ppermute | solution.py:22
  101.5 17.9 %collective-permute-start.33 = (bf16[1,28,256]{2,1,0:T(8,128)(2,1)}, bf16[1,28,256]{2,1,0:T(8,128)(2,1)S(1)}, u32[]{:S(2)}, u32[]{:S(2)}) collective-permute-start(bf16[1,28,256]{2,1,0:T(8,128)(2,1)} %get-tuple-element.101), channel_id=1, source_target_pairs={{8,0},{16,8},{24,16},{32,24},{40,32},{48,40},{56,48},{64,56},{72,6... | collective-permute-start | bytes 43016 | tf_op jit(solution)/shard_map/ppermute | solution.py:22
  105.8 18.2 %collective-permute-start.50 = (bf16[1,28,256]{2,1,0:T(8,128)(2,1)S(1)}, bf16[1,28,256]{2,1,0:T(8,128)(2,1)S(1)}, u32[]{:S(2)}, u32[]{:S(2)}) collective-permute-start(bf16[1,28,256]{2,1,0:T(8,128)(2,1)S(1)} %get-tuple-element.98), channel_id=1, source_target_pairs={{0,8},{8,16},{16,24},{24,32},{32,40},{40,48},{48,56},{56,64},{64,7... | collective-permute-start | bytes 43016 | tf_op jit(solution)/shard_map/ppermute | solution.py:22
  107.7 18.1 %collective-permute-start.53 = (bf16[1,28,256]{2,1,0:T(8,128)(2,1)S(1)}, bf16[1,28,256]{2,1,0:T(8,128)(2,1)S(1)}, u32[]{:S(2)}, u32[]{:S(2)}) collective-permute-start(bf16[1,28,256]{2,1,0:T(8,128)(2,1)S(1)} %get-tuple-element.96), channel_id=1, source_target_pairs={{0,1},{1,2},{2,3},{3,4},{4,5},{5,6},{6,7},{8,9},{9,10},{10,11},{11... | collective-permute-start | bytes 43016 | tf_op jit(solution)/shard_map/ppermute | solution.py:22
  111.7 16.1 %collective-permute-start.54 = (bf16[1,28,256]{2,1,0:T(8,128)(2,1)S(1)}, bf16[1,28,256]{2,1,0:T(8,128)(2,1)S(1)}, u32[]{:S(2)}, u32[]{:S(2)}) collective-permute-start(bf16[1,28,256]{2,1,0:T(8,128)(2,1)S(1)} %get-tuple-element.95), channel_id=1, source_target_pairs={{1,0},{2,1},{3,2},{4,3},{5,4},{6,5},{7,6},{9,8},{10,9},{11,10},{12... | collective-permute-start | bytes 43016 | tf_op jit(solution)/shard_map/ppermute | solution.py:22
  113.6 16.1 %collective-permute-start.57 = (bf16[1,28,256]{2,1,0:T(8,128)(2,1)S(1)}, bf16[1,28,256]{2,1,0:T(8,128)(2,1)S(1)}, u32[]{:S(2)}, u32[]{:S(2)}) collective-permute-start(bf16[1,28,256]{2,1,0:T(8,128)(2,1)S(1)} %get-tuple-element.93), channel_id=1, source_target_pairs={{8,0},{16,8},{24,16},{32,24},{40,32},{48,40},{56,48},{64,56},{72,6... | collective-permute-start | bytes 43016 | tf_op jit(solution)/shard_map/ppermute | solution.py:22
  124.0 36.8 %collective-permute-start.24 = (bf16[1,28,256]{2,1,0:T(8,128)(2,1)S(1)}, bf16[1,28,256]{2,1,0:T(8,128)(2,1)}, u32[]{:S(2)}, u32[]{:S(2)}) collective-permute-start(bf16[1,28,256]{2,1,0:T(8,128)(2,1)S(1)} %get-tuple-element.107), channel_id=1, source_target_pairs={{0,8},{8,16},{16,24},{24,32},{32,40},{40,48},{48,56},{56,64},{64,7... | collective-permute-start | bytes 43016 | tf_op jit(solution)/shard_map/ppermute | solution.py:22
  125.9 36.8 %collective-permute-start.27 = (bf16[1,28,256]{2,1,0:T(8,128)(2,1)S(1)}, bf16[1,28,256]{2,1,0:T(8,128)(2,1)}, u32[]{:S(2)}, u32[]{:S(2)}) collective-permute-start(bf16[1,28,256]{2,1,0:T(8,128)(2,1)S(1)} %get-tuple-element.105), channel_id=1, source_target_pairs={{0,8},{8,16},{16,24},{24,32},{32,40},{40,48},{48,56},{56,64},{64,7... | collective-permute-start | bytes 43016 | tf_op jit(solution)/shard_map/ppermute | solution.py:22
  127.8 22.5 %collective-permute-start.4 = (bf16[1,28,256]{2,1,0:T(8,128)(2,1)}, bf16[1,28,256]{2,1,0:T(8,128)(2,1)}, u32[]{:S(2)}, u32[]{:S(2)}) collective-permute-start(bf16[1,28,256]{2,1,0:T(8,128)(2,1)} %collective-permute-done.3), channel_id=1, source_target_pairs={{1,0},{2,1},{3,2},{4,3},{5,4},{6,5},{7,6},{9,8},{10,9},{11,10},{12... | collective-permute-start | bytes 43016 | tf_op jit(solution)/shard_map/ppermute | solution.py:22
  129.8 26.8 %collective-permute-start.8 = (bf16[1,28,256]{2,1,0:T(8,128)(2,1)}, bf16[1,28,256]{2,1,0:T(8,128)(2,1)}, u32[]{:S(2)}, u32[]{:S(2)}) collective-permute-start(bf16[1,28,256]{2,1,0:T(8,128)(2,1)} %collective-permute-done.7), channel_id=1, source_target_pairs={{0,1},{1,2},{2,3},{3,4},{4,5},{5,6},{6,7},{8,9},{9,10},{10,11},{11... | collective-permute-start | bytes 43016 | tf_op jit(solution)/shard_map/ppermute | solution.py:22
  133.5 33.7 %collective-permute-start.11 = (bf16[1,28,256]{2,1,0:T(8,128)(2,1)}, bf16[1,28,256]{2,1,0:T(8,128)(2,1)S(1)}, u32[]{:S(2)}, u32[]{:S(2)}) collective-permute-start(bf16[1,28,256]{2,1,0:T(8,128)(2,1)} %collective-permute-done.10), channel_id=1, source_target_pairs={{1,0},{2,1},{3,2},{4,3},{5,4},{6,5},{7,6},{9,8},{10,9},{11,10},{12... | collective-permute-start | bytes 43016 | tf_op jit(solution)/shard_map/ppermute | solution.py:22
  150.4 59.4 %collective-permute-start.31 = (bf16[1,28,256]{2,1,0:T(8,128)(2,1)}, bf16[1,28,256]{2,1,0:T(8,128)(2,1)}, u32[]{:S(2)}, u32[]{:S(2)}) collective-permute-start(bf16[1,28,256]{2,1,0:T(8,128)(2,1)} %get-tuple-element.102), channel_id=1, source_target_pairs={{8,0},{16,8},{24,16},{32,24},{40,32},{48,40},{56,48},{64,56},{72,6... | collective-permute-start | bytes 43016 | tf_op jit(solution)/shard_map/ppermute | solution.py:22
  156.6 55.2 %collective-permute-start.34 = (bf16[1,28,256]{2,1,0:T(8,128)(2,1)}, bf16[1,28,256]{2,1,0:T(8,128)(2,1)}, u32[]{:S(2)}, u32[]{:S(2)}) collective-permute-start(bf16[1,28,256]{2,1,0:T(8,128)(2,1)} %get-tuple-element.100), channel_id=1, source_target_pairs={{8,0},{16,8},{24,16},{32,24},{40,32},{48,40},{56,48},{64,56},{72,6... | collective-permute-start | bytes 43016 | tf_op jit(solution)/shard_map/ppermute | solution.py:22
  160.8 56.6 %collective-permute-start.48 = (bf16[1,28,256]{2,1,0:T(8,128)(2,1)}, bf16[1,28,256]{2,1,0:T(8,128)(2,1)}, u32[]{:S(2)}, u32[]{:S(2)}) collective-permute-start(bf16[1,28,256]{2,1,0:T(8,128)(2,1)} %get-tuple-element.99), channel_id=1, source_target_pairs={{0,8},{8,16},{16,24},{24,32},{32,40},{40,48},{48,56},{56,64},{64,7... | collective-permute-start | bytes 43016 | tf_op jit(solution)/shard_map/ppermute | solution.py:22
  162.7 58.0 %collective-permute-start.25 = (bf16[1,28,256]{2,1,0:T(8,128)(2,1)}, bf16[1,28,256]{2,1,0:T(8,128)(2,1)}, u32[]{:S(2)}, u32[]{:S(2)}) collective-permute-start(bf16[1,28,256]{2,1,0:T(8,128)(2,1)} %collective-permute-done.24), channel_id=1, source_target_pairs={{0,1},{1,2},{2,3},{3,4},{4,5},{5,6},{6,7},{8,9},{9,10},{10,11},{11... | collective-permute-start | bytes 43016 | tf_op jit(solution)/shard_map/ppermute | solution.py:22
  167.2 58.0 %collective-permute-start.28 = (bf16[1,28,256]{2,1,0:T(8,128)(2,1)}, bf16[1,28,256]{2,1,0:T(8,128)(2,1)}, u32[]{:S(2)}, u32[]{:S(2)}) collective-permute-start(bf16[1,28,256]{2,1,0:T(8,128)(2,1)} %collective-permute-done.27), channel_id=1, source_target_pairs={{1,0},{2,1},{3,2},{4,3},{5,4},{6,5},{7,6},{9,8},{10,9},{11,10},{12... | collective-permute-start | bytes 43016 | tf_op jit(solution)/shard_map/ppermute | solution.py:22
  209.8 22.4 %collective-permute-start.51 = (bf16[1,28,256]{2,1,0:T(8,128)(2,1)}, bf16[1,28,256]{2,1,0:T(8,128)(2,1)}, u32[]{:S(2)}, u32[]{:S(2)}) collective-permute-start(bf16[1,28,256]{2,1,0:T(8,128)(2,1)} %get-tuple-element.97), channel_id=1, source_target_pairs={{0,8},{8,16},{16,24},{24,32},{32,40},{40,48},{48,56},{56,64},{64,7... | collective-permute-start | bytes 43016 | tf_op jit(solution)/shard_map/ppermute | solution.py:22
  211.8 24.0 %collective-permute-start.55 = (bf16[1,28,256]{2,1,0:T(8,128)(2,1)}, bf16[1,28,256]{2,1,0:T(8,128)(2,1)}, u32[]{:S(2)}, u32[]{:S(2)}) collective-permute-start(bf16[1,28,256]{2,1,0:T(8,128)(2,1)} %get-tuple-element.94), channel_id=1, source_target_pairs={{8,0},{16,8},{24,16},{32,24},{40,32},{48,40},{56,48},{64,56},{72,6... | collective-permute-start | bytes 43016 | tf_op jit(solution)/shard_map/ppermute | solution.py:22
  217.3 20.4 %collective-permute-start.58 = (bf16[1,28,256]{2,1,0:T(8,128)(2,1)}, bf16[1,28,256]{2,1,0:T(8,128)(2,1)}, u32[]{:S(2)}, u32[]{:S(2)}) collective-permute-start(bf16[1,28,256]{2,1,0:T(8,128)(2,1)} %get-tuple-element.92), channel_id=1, source_target_pairs={{8,0},{16,8},{24,16},{32,24},{40,32},{48,40},{56,48},{64,56},{72,6... | collective-permute-start | bytes 43016 | tf_op jit(solution)/shard_map/ppermute | solution.py:22
  220.7 20.7 %collective-permute-start.32 = (bf16[1,28,256]{2,1,0:T(8,128)(2,1)}, bf16[1,28,256]{2,1,0:T(8,128)(2,1)S(1)}, u32[]{:S(2)}, u32[]{:S(2)}) collective-permute-start(bf16[1,28,256]{2,1,0:T(8,128)(2,1)} %collective-permute-done.31), channel_id=1, source_target_pairs={{0,1},{1,2},{2,3},{3,4},{4,5},{5,6},{6,7},{8,9},{9,10},{10,11},{11... | collective-permute-start | bytes 43016 | tf_op jit(solution)/shard_map/ppermute | solution.py:22
  225.2 18.2 %collective-permute-start.35 = (bf16[1,28,256]{2,1,0:T(8,128)(2,1)}, bf16[1,28,256]{2,1,0:T(8,128)(2,1)S(1)}, u32[]{:S(2)}, u32[]{:S(2)}) collective-permute-start(bf16[1,28,256]{2,1,0:T(8,128)(2,1)} %collective-permute-done.34), channel_id=1, source_target_pairs={{1,0},{2,1},{3,2},{4,3},{5,4},{6,5},{7,6},{9,8},{10,9},{11,10},{12... | collective-permute-start | bytes 43016 | tf_op jit(solution)/shard_map/ppermute | solution.py:22
  232.1 34.7 %collective-permute-start.49 = (bf16[1,28,256]{2,1,0:T(8,128)(2,1)}, bf16[1,28,256]{2,1,0:T(8,128)(2,1)}, u32[]{:S(2)}, u32[]{:S(2)}) collective-permute-start(bf16[1,28,256]{2,1,0:T(8,128)(2,1)} %collective-permute-done.48), channel_id=1, source_target_pairs={{0,1},{1,2},{2,3},{3,4},{4,5},{5,6},{6,7},{8,9},{9,10},{10,11},{11... | collective-permute-start | bytes 43016 | tf_op jit(solution)/shard_map/ppermute | solution.py:22
  235.8 33.7 %collective-permute-start.52 = (bf16[1,28,256]{2,1,0:T(8,128)(2,1)}, bf16[1,28,256]{2,1,0:T(8,128)(2,1)}, u32[]{:S(2)}, u32[]{:S(2)}) collective-permute-start(bf16[1,28,256]{2,1,0:T(8,128)(2,1)} %collective-permute-done.51), channel_id=1, source_target_pairs={{1,0},{2,1},{3,2},{4,3},{5,4},{6,5},{7,6},{9,8},{10,9},{11,10},{12... | collective-permute-start | bytes 43016 | tf_op jit(solution)/shard_map/ppermute | solution.py:22
  237.7 35.5 %collective-permute-start.56 = (bf16[1,28,256]{2,1,0:T(8,128)(2,1)}, bf16[1,28,256]{2,1,0:T(8,128)(2,1)}, u32[]{:S(2)}, u32[]{:S(2)}) collective-permute-start(bf16[1,28,256]{2,1,0:T(8,128)(2,1)} %collective-permute-done.55), channel_id=1, source_target_pairs={{0,1},{1,2},{2,3},{3,4},{4,5},{5,6},{6,7},{8,9},{9,10},{10,11},{11... | collective-permute-start | bytes 43016 | tf_op jit(solution)/shard_map/ppermute | solution.py:22
  241.4 37.0 %collective-permute-start.59 = (bf16[1,28,256]{2,1,0:T(8,128)(2,1)}, bf16[1,28,256]{2,1,0:T(8,128)(2,1)}, u32[]{:S(2)}, u32[]{:S(2)}) collective-permute-start(bf16[1,28,256]{2,1,0:T(8,128)(2,1)} %collective-permute-done.58), channel_id=1, source_target_pairs={{1,0},{2,1},{3,2},{4,3},{5,4},{6,5},{7,6},{9,8},{10,9},{11,10},{12... | collective-permute-start | bytes 43016 | tf_op jit(solution)/shard_map/ppermute | solution.py:22
  243.4 55.2 %collective-permute-start.12 = (f32[28,256]{1,0:T(8,128)}, f32[28,256]{1,0:T(8,128)}, u32[]{:S(2)}, u32[]{:S(2)}) collective-permute-start(f32[28,256]{1,0:T(8,128)} %bitcast.43), channel_id=1, source_target_pairs={{0,8},{8,16},{16,24},{24,32},{32,40},{40,48},{48,56},{56,64},{64,7... | collective-permute-start | bytes 86024 | tf_op jit(solution)/shard_map/ppermute | solution.py:22
  266.8 35.9 %collective-permute-start.14 = (f32[28,256]{1,0:T(8,128)}, f32[28,256]{1,0:T(8,128)}, u32[]{:S(2)}, u32[]{:S(2)}) collective-permute-start(f32[28,256]{1,0:T(8,128)} %bitcast.44), channel_id=1, source_target_pairs={{0,8},{8,16},{16,24},{24,32},{32,40},{40,48},{48,56},{56,64},{64,7... | collective-permute-start | bytes 86024 | tf_op jit(solution)/shard_map/ppermute | solution.py:22
  269.5 37.7 %collective-permute-start.15 = (f32[28,256]{1,0:T(8,128)}, f32[28,256]{1,0:T(8,128)}, u32[]{:S(2)}, u32[]{:S(2)}) collective-permute-start(f32[28,256]{1,0:T(8,128)} %bitcast.45), channel_id=1, source_target_pairs={{0,8},{8,16},{16,24},{24,32},{32,40},{40,48},{48,56},{56,64},{64,7... | collective-permute-start | bytes 86024 | tf_op jit(solution)/shard_map/ppermute | solution.py:22
  273.2 37.3 %collective-permute-start.17 = (f32[28,256]{1,0:T(8,128)}, f32[28,256]{1,0:T(8,128)}, u32[]{:S(2)}, u32[]{:S(2)}) collective-permute-start(f32[28,256]{1,0:T(8,128)} %bitcast.46), channel_id=1, source_target_pairs={{0,1},{1,2},{2,3},{3,4},{4,5},{5,6},{6,7},{8,9},{9,10},{10,11},{11... | collective-permute-start | bytes 86024 | tf_op jit(solution)/shard_map/ppermute | solution.py:22
  278.4 36.6 %collective-permute-start.18 = (f32[28,256]{1,0:T(8,128)}, f32[28,256]{1,0:T(8,128)}, u32[]{:S(2)}, u32[]{:S(2)}) collective-permute-start(f32[28,256]{1,0:T(8,128)} %bitcast.47), channel_id=1, source_target_pairs={{1,0},{2,1},{3,2},{4,3},{5,4},{6,5},{7,6},{9,8},{10,9},{11,10},{12... | collective-permute-start | bytes 86024 | tf_op jit(solution)/shard_map/ppermute | solution.py:22
  298.6 18.4 %collective-permute-start.19 = (f32[28,256]{1,0:T(8,128)S(1)}, f32[28,256]{1,0:T(8,128)}, u32[]{:S(2)}, u32[]{:S(2)}) collective-permute-start(f32[28,256]{1,0:T(8,128)S(1)} %bitcast.405), channel_id=1, source_target_pairs={{8,0},{16,8},{24,16},{32,24},{40,32},{48,40},{56,48},{64,56},{72,6... | collective-permute-start | bytes 86024 | tf_op jit(solution)/shard_map/ppermute | solution.py:22
  302.8 17.8 %collective-permute-start.22 = (f32[28,256]{1,0:T(8,128)S(1)}, f32[28,256]{1,0:T(8,128)}, u32[]{:S(2)}, u32[]{:S(2)}) collective-permute-start(f32[28,256]{1,0:T(8,128)S(1)} %bitcast.404), channel_id=1, source_target_pairs={{8,0},{16,8},{24,16},{32,24},{40,32},{48,40},{56,48},{64,56},{72,6... | collective-permute-start | bytes 86024 | tf_op jit(solution)/shard_map/ppermute | solution.py:22
  307.2 26.7 %collective-permute-start.21 = (f32[28,256]{1,0:T(8,128)}, f32[28,256]{1,0:T(8,128)S(1)}, u32[]{:S(2)}, u32[]{:S(2)}) collective-permute-start(f32[28,256]{1,0:T(8,128)} %bitcast.49), channel_id=1, source_target_pairs={{8,0},{16,8},{24,16},{32,24},{40,32},{48,40},{56,48},{64,56},{72,6... | collective-permute-start | bytes 86024 | tf_op jit(solution)/shard_map/ppermute | solution.py:22
  310.5 23.4 %collective-permute-start.13 = (f32[28,256]{1,0:T(8,128)}, f32[28,256]{1,0:T(8,128)S(1)}, u32[]{:S(2)}, u32[]{:S(2)}) collective-permute-start(f32[28,256]{1,0:T(8,128)} %collective-permute-done.12), channel_id=1, source_target_pairs={{0,1},{1,2},{2,3},{3,4},{4,5},{5,6},{6,7},{8,9},{9,10},{10,11},{11... | collective-permute-start | bytes 86024 | tf_op jit(solution)/shard_map/ppermute | solution.py:22
  315.0 18.9 %collective-permute-start.16 = (f32[28,256]{1,0:T(8,128)}, f32[28,256]{1,0:T(8,128)S(1)}, u32[]{:S(2)}, u32[]{:S(2)}) collective-permute-start(f32[28,256]{1,0:T(8,128)} %collective-permute-done.15), channel_id=1, source_target_pairs={{1,0},{2,1},{3,2},{4,3},{5,4},{6,5},{7,6},{9,8},{10,9},{11,10},{12... | collective-permute-start | bytes 86024 | tf_op jit(solution)/shard_map/ppermute | solution.py:22
  317.0 17.0 %collective-permute-start.20 = (f32[28,256]{1,0:T(8,128)}, f32[28,256]{1,0:T(8,128)S(1)}, u32[]{:S(2)}, u32[]{:S(2)}) collective-permute-start(f32[28,256]{1,0:T(8,128)} %collective-permute-done.19), channel_id=1, source_target_pairs={{0,1},{1,2},{2,3},{3,4},{4,5},{5,6},{6,7},{8,9},{9,10},{10,11},{11... | collective-permute-start | bytes 86024 | tf_op jit(solution)/shard_map/ppermute | solution.py:22
  383.9 26.3 %collective-permute-start.36 = (f32[28,256]{1,0:T(8,128)}, f32[28,256]{1,0:T(8,128)}, u32[]{:S(2)}, u32[]{:S(2)}) collective-permute-start(f32[28,256]{1,0:T(8,128)} %bitcast.81), channel_id=1, source_target_pairs={{0,8},{8,16},{16,24},{24,32},{32,40},{40,48},{48,56},{56,64},{64,7... | collective-permute-start | bytes 86024 | tf_op jit(solution)/shard_map/ppermute | solution.py:22
  387.4 26.9 %collective-permute-start.38 = (f32[28,256]{1,0:T(8,128)}, f32[28,256]{1,0:T(8,128)}, u32[]{:S(2)}, u32[]{:S(2)}) collective-permute-start(f32[28,256]{1,0:T(8,128)} %bitcast.82), channel_id=1, source_target_pairs={{0,8},{8,16},{16,24},{24,32},{32,40},{40,48},{48,56},{56,64},{64,7... | collective-permute-start | bytes 86024 | tf_op jit(solution)/shard_map/ppermute | solution.py:22
  390.9 29.9 %collective-permute-start.39 = (f32[28,256]{1,0:T(8,128)}, f32[28,256]{1,0:T(8,128)}, u32[]{:S(2)}, u32[]{:S(2)}) collective-permute-start(f32[28,256]{1,0:T(8,128)} %bitcast.83), channel_id=1, source_target_pairs={{0,8},{8,16},{16,24},{24,32},{32,40},{40,48},{48,56},{56,64},{64,7... | collective-permute-start | bytes 86024 | tf_op jit(solution)/shard_map/ppermute | solution.py:22
  395.5 28.6 %collective-permute-start.41 = (f32[28,256]{1,0:T(8,128)}, f32[28,256]{1,0:T(8,128)}, u32[]{:S(2)}, u32[]{:S(2)}) collective-permute-start(f32[28,256]{1,0:T(8,128)} %bitcast.84), channel_id=1, source_target_pairs={{0,1},{1,2},{2,3},{3,4},{4,5},{5,6},{6,7},{8,9},{9,10},{10,11},{11... | collective-permute-start | bytes 86024 | tf_op jit(solution)/shard_map/ppermute | solution.py:22
  400.9 27.7 %collective-permute-start.42 = (f32[28,256]{1,0:T(8,128)S(1)}, f32[28,256]{1,0:T(8,128)}, u32[]{:S(2)}, u32[]{:S(2)}) collective-permute-start(f32[28,256]{1,0:T(8,128)S(1)} %bitcast.403), channel_id=1, source_target_pairs={{1,0},{2,1},{3,2},{4,3},{5,4},{6,5},{7,6},{9,8},{10,9},{11,10},{12... | collective-permute-start | bytes 86024 | tf_op jit(solution)/shard_map/ppermute | solution.py:22
  410.2 20.4 %collective-permute-start.43 = (f32[28,256]{1,0:T(8,128)}, f32[28,256]{1,0:T(8,128)}, u32[]{:S(2)}, u32[]{:S(2)}) collective-permute-start(f32[28,256]{1,0:T(8,128)} %bitcast.86), channel_id=1, source_target_pairs={{8,0},{16,8},{24,16},{32,24},{40,32},{48,40},{56,48},{64,56},{72,6... | collective-permute-start | bytes 86024 | tf_op jit(solution)/shard_map/ppermute | solution.py:22
  414.3 19.9 %collective-permute-start.46 = (f32[28,256]{1,0:T(8,128)}, f32[28,256]{1,0:T(8,128)}, u32[]{:S(2)}, u32[]{:S(2)}) collective-permute-start(f32[28,256]{1,0:T(8,128)} %bitcast.88), channel_id=1, source_target_pairs={{8,0},{16,8},{24,16},{32,24},{40,32},{48,40},{56,48},{64,56},{72,6... | collective-permute-start | bytes 86024 | tf_op jit(solution)/shard_map/ppermute | solution.py:22
  420.8 23.2 %collective-permute-start.45 = (f32[28,256]{1,0:T(8,128)}, f32[28,256]{1,0:T(8,128)}, u32[]{:S(2)}, u32[]{:S(2)}) collective-permute-start(f32[28,256]{1,0:T(8,128)} %bitcast.87), channel_id=1, source_target_pairs={{8,0},{16,8},{24,16},{32,24},{40,32},{48,40},{56,48},{64,56},{72,6... | collective-permute-start | bytes 86024 | tf_op jit(solution)/shard_map/ppermute | solution.py:22
  424.1 20.7 %collective-permute-start.37 = (f32[28,256]{1,0:T(8,128)}, f32[28,256]{1,0:T(8,128)}, u32[]{:S(2)}, u32[]{:S(2)}) collective-permute-start(f32[28,256]{1,0:T(8,128)} %collective-permute-done.36), channel_id=1, source_target_pairs={{0,1},{1,2},{2,3},{3,4},{4,5},{5,6},{6,7},{8,9},{9,10},{10,11},{11... | collective-permute-start | bytes 86024 | tf_op jit(solution)/shard_map/ppermute | solution.py:22
  428.6 16.9 %collective-permute-start.40 = (f32[28,256]{1,0:T(8,128)}, f32[28,256]{1,0:T(8,128)}, u32[]{:S(2)}, u32[]{:S(2)}) collective-permute-start(f32[28,256]{1,0:T(8,128)} %collective-permute-done.39), channel_id=1, source_target_pairs={{1,0},{2,1},{3,2},{4,3},{5,4},{6,5},{7,6},{9,8},{10,9},{11,10},{12... | collective-permute-start | bytes 86024 | tf_op jit(solution)/shard_map/ppermute | solution.py:22
  430.6 15.8 %collective-permute-start.44 = (f32[28,256]{1,0:T(8,128)}, f32[28,256]{1,0:T(8,128)}, u32[]{:S(2)}, u32[]{:S(2)}) collective-permute-start(f32[28,256]{1,0:T(8,128)} %collective-permute-done.43), channel_id=1, source_target_pairs={{0,1},{1,2},{2,3},{3,4},{4,5},{5,6},{6,7},{8,9},{9,10},{10,11},{11... | collective-permute-start | bytes 86024 | tf_op jit(solution)/shard_map/ppermute | solution.py:22
  495.6 98.8 %collective-permute-start.60 = (f32[28,256]{1,0:T(8,128)}, f32[28,256]{1,0:T(8,128)}, u32[]{:S(2)}, u32[]{:S(2)}) collective-permute-start(f32[28,256]{1,0:T(8,128)} %bitcast.119), channel_id=1, source_target_pairs={{0,8},{8,16},{16,24},{24,32},{32,40},{40,48},{48,56},{56,64},{64,7... | collective-permute-start | bytes 86024 | tf_op jit(solution)/shard_map/ppermute | solution.py:22
  499.1 99.4 %collective-permute-start.62 = (f32[28,256]{1,0:T(8,128)}, f32[28,256]{1,0:T(8,128)}, u32[]{:S(2)}, u32[]{:S(2)}) collective-permute-start(f32[28,256]{1,0:T(8,128)} %bitcast.120), channel_id=1, source_target_pairs={{0,8},{8,16},{16,24},{24,32},{32,40},{40,48},{48,56},{56,64},{64,7... | collective-permute-start | bytes 86024 | tf_op jit(solution)/shard_map/ppermute | solution.py:22
  502.6 100.7 %collective-permute-start.63 = (f32[28,256]{1,0:T(8,128)}, f32[28,256]{1,0:T(8,128)}, u32[]{:S(2)}, u32[]{:S(2)}) collective-permute-start(f32[28,256]{1,0:T(8,128)} %bitcast.121), channel_id=1, source_target_pairs={{0,8},{8,16},{16,24},{24,32},{32,40},{40,48},{48,56},{56,64},{64,7... | collective-permute-start | bytes 86024 | tf_op jit(solution)/shard_map/ppermute | solution.py:22
  506.5 99.3 %collective-permute-start.65 = (f32[28,256]{1,0:T(8,128)}, f32[28,256]{1,0:T(8,128)}, u32[]{:S(2)}, u32[]{:S(2)}) collective-permute-start(f32[28,256]{1,0:T(8,128)} %bitcast.122), channel_id=1, source_target_pairs={{0,1},{1,2},{2,3},{3,4},{4,5},{5,6},{6,7},{8,9},{9,10},{10,11},{11... | collective-permute-start | bytes 86024 | tf_op jit(solution)/shard_map/ppermute | solution.py:22
  511.0 96.8 %collective-permute-start.66 = (f32[28,256]{1,0:T(8,128)S(1)}, f32[28,256]{1,0:T(8,128)}, u32[]{:S(2)}, u32[]{:S(2)}) collective-permute-start(f32[28,256]{1,0:T(8,128)S(1)} %bitcast.402), channel_id=1, source_target_pairs={{1,0},{2,1},{3,2},{4,3},{5,4},{6,5},{7,6},{9,8},{10,9},{11,10},{12... | collective-permute-start | bytes 86024 | tf_op jit(solution)/shard_map/ppermute | solution.py:22
  594.4 15.8 %collective-permute-start.67 = (f32[28,256]{1,0:T(8,128)}, f32[28,256]{1,0:T(8,128)}, u32[]{:S(2)}, u32[]{:S(2)}) collective-permute-start(f32[28,256]{1,0:T(8,128)} %bitcast.124), channel_id=1, source_target_pairs={{8,0},{16,8},{24,16},{32,24},{40,32},{48,40},{56,48},{64,56},{72,6... | collective-permute-start | bytes 86024 | tf_op jit(solution)/shard_map/ppermute | solution.py:22
  603.4 19.9 %collective-permute-start.69 = (f32[28,256]{1,0:T(8,128)}, f32[28,256]{1,0:T(8,128)S(1)}, u32[]{:S(2)}, u32[]{:S(2)}) collective-permute-start(f32[28,256]{1,0:T(8,128)} %bitcast.125), channel_id=1, source_target_pairs={{8,0},{16,8},{24,16},{32,24},{40,32},{48,40},{56,48},{64,56},{72,6... | collective-permute-start | bytes 86024 | tf_op jit(solution)/shard_map/ppermute | solution.py:22
  605.8 17.4 %collective-permute-start.61 = (f32[28,256]{1,0:T(8,128)}, f32[28,256]{1,0:T(8,128)S(1)}, u32[]{:S(2)}, u32[]{:S(2)}) collective-permute-start(f32[28,256]{1,0:T(8,128)} %collective-permute-done.60), channel_id=1, source_target_pairs={{0,1},{1,2},{2,3},{3,4},{4,5},{5,6},{6,7},{8,9},{9,10},{10,11},{11... | collective-permute-start | bytes 86024 | tf_op jit(solution)/shard_map/ppermute | solution.py:22
  607.8 15.4 %collective-permute-start.64 = (f32[28,256]{1,0:T(8,128)}, f32[28,256]{1,0:T(8,128)S(1)}, u32[]{:S(2)}, u32[]{:S(2)}) collective-permute-start(f32[28,256]{1,0:T(8,128)} %collective-permute-done.63), channel_id=1, source_target_pairs={{1,0},{2,1},{3,2},{4,3},{5,4},{6,5},{7,6},{9,8},{10,9},{11,10},{12... | collective-permute-start | bytes 86024 | tf_op jit(solution)/shard_map/ppermute | solution.py:22
  (161 other events, 2199.5 us)
where the time goes:
time: 654 us; the launch traced here: 642 us
  starting transfers between devices  218 us (33%)
  local copies, waits for them, and re-layouts  197 us (30%)
  other arithmetic  143 us (22%)
  blocking collectives  70.7 us (11%)
  matrix products  7.69 us (1%)
    ppermute x72, starting transfers between devices, shifted(): return lax.ppermute(x, axis, pairs)  218 us
    psum x1, blocking collectives, local(): lax.psum(terms, ('gx', 'gy'))  70.7 us
    scatter-add x3, other arithmetic, local_operator(): trace_table[:, partner.reshape(-1)].reshape(channels, 3, element_count)  53.6 us
    scatter-add x3, other arithmetic, section_adjoint(): flat_bar = jnp.zeros((channels, 3 * element_count), jnp.float32).at[:, fa...  41.3 us
    gather x6, local copies, waits for them, and re-layouts, section_adjoint(): outer_forward = trace_table[:, partner.reshape(-1)]  40.6 us
    unnamed x343, local copies, waits for them, and re-layouts  36.6 us
    gather x6, local copies, waits for them, and re-layouts, section_received(): flat_states[:, :, faces_sent] * live_slots[None, None]  29 us
    another operation x54, local copies, waits for them, and re-layouts, route_blocks(): return jnp.stack(pieces, axis=-2)  28.7 us
  transfers between devices with their start and end apart: 72, of which 0 were waited for; matrix products, arithmetic and copies ran while one was open for 29% of the time, Pallas kernels for 0%

commit v1 on v0

v1 whole, which is shorter than its diff:
```python
import jax
import jax.numpy as jnp
from jax import lax
from jax.experimental import pallas as pl
from jax.experimental.pallas import tpu as pltpu
from jax.sharding import PartitionSpec as P

GX, GY = 16, 8
COMPS = 14
QCOMP, ZCOMP = 14, 15
ZONES = 512
DT = 0.2
GRAD_WEIGHT = 1.0 / 64.0
FACE_NODES = ((1, 2), (2, 0), (0, 1))
MAIN = (1, 3, 4, 6)
DIAG = (0, 2, 5, 7)
STEPS = ((-1, -1), (-1, 0), (-1, 1), (0, -1), (0, 1), (1, -1), (1, 0), (1, 1))
WINDOW, BEHIND = 80, 36
MESH = pl.DeviceIdType.MESH
TILE = (8, 128)
F32 = jnp.float32


def take(x, idx):
    return jnp.take_along_axis(x, idx, axis=1, mode="promise_in_bounds")


def row(ref, *at):
    return jnp.broadcast_to(ref[at], TILE)


def pick(code, values, like):
    out = jnp.full(TILE, values[-1], like.dtype)
    for i in range(len(values) - 2, -1, -1):
        out = jnp.where(code == i, values[i], out)
    return out


def ends(nodes, is0, is1):
    a, b, c = nodes
    first = jnp.where(is0, b, jnp.where(is1, c, a))
    second = jnp.where(is0, c, jnp.where(is1, a, b))
    return first, second


def kernel(
    cot, states, area_ref, edge_ref, rough_ref, soil_ref, zf_ref, zc_ref, wet_ref, zone_ref, send_ref, partner_ref,
    vol, fin, fout,
    out, grads,
    tab, aux, xs, local, pre, lam, kept, sbuf, rbuf, sdiag, rdiag, cdiag, gyb, gxb,
    send_sem, recv_sem, gy_send, gy_recv, gx_send, gx_recv,
):
    ix, iy = lax.axis_index("gx"), lax.axis_index("gy")

    def at(dx, dy):
        return (lax.rem(ix + dx + GX, GX), lax.rem(iy + dy + GY, GY))

    barrier = pltpu.get_barrier_semaphore()
    peers = [at(*STEPS[n]) for n in DIAG]
    peers += [at(0, k) for k in range(1, GY)]
    peers += [at(k, 0) for k in range(1, GX)]
    for peer in peers:
        pl.semaphore_signal(barrier, inc=1, device_id=peer, device_id_type=MESH)

    sub = lax.broadcasted_iota(jnp.int32, TILE, 0)
    lane = lax.broadcasted_iota(jnp.int32, TILE, 1)

    area = area_ref[...]
    rough = rough_ref[...]
    wet = wet_ref[...].astype(F32)
    zone = zone_ref[...]
    edge = [edge_ref[f] for f in range(3)]
    kappa = jnp.zeros(TILE, F32)
    zfric = jnp.zeros(TILE, F32)
    zlo, zhi = zone & 127, zone >> 7
    for t in range(4):
        kappa = jnp.where(zhi == t, take(row(zc_ref, pl.ds(t, 1)), zlo), kappa)
        zfric = jnp.where(zhi == t, take(row(zf_ref, pl.ds(t, 1)), zlo), zfric)
    kappa = kappa * soil_ref[...]
    half_kappa = 0.5 * kappa
    rough_zone = zfric * rough

    slots = jnp.concatenate(
        [send_ref[n : n + 1, h * 128 : (h + 1) * 128] for n in MAIN for h in range(2)], axis=0
    )
    m_lo, m_hi, m_f = slots & 127, (slots >> 7) & 7, slots >> 10
    m_is0, m_is1 = m_f == 0, m_f == 1
    dslots = jnp.zeros(TILE, jnp.int32)
    for i, n in enumerate(DIAG):
        first = jnp.broadcast_to(send_ref[n : n + 1, 0:128], TILE)
        d = 3 - i
        moved = pltpu.roll(first, 4 * d, axis=1) if d else first
        dslots = jnp.where((lane >> 2) == d, moved, dslots)
    d_lo, d_hi, d_f = dslots & 127, (dslots >> 7) & 7, dslots >> 10
    d_is0, d_is1 = d_f == 0, d_f == 1

    p_lo, p_loc, p_rem, p_is0, p_is1 = [], [], [], [], []
    for f in range(3):
        p = partner_ref[f]
        there = p - 3072
        n = there >> 8
        slot_row = pick(n, (8, 0, 8, 2, 4, 8, 6, 8), p) + ((there >> 7) & 1)
        is_diag = (n == 0) | (n == 2) | (n == 5) | (n == 7)
        far = p >= 3072
        d_lane = pick(n, (0, 0, 4, 0, 0, 8, 0, 12), p) + (p & 3)
        p_lo.append(jnp.where(far & is_diag, d_lane, p & 127))
        p_loc.append(jnp.where(far, -1, (p >> 7) & 7))
        p_rem.append(jnp.where(far, jnp.where(is_diag, 8, slot_row), -1))
        p_is0.append((p >> 10) == 0)
        p_is1.append((p >> 10) == 1)

    def from_slots(ref, c):
        nodes = []
        for n in range(3):
            acc = jnp.zeros(TILE, F32)
            for s in range(8):
                acc = jnp.where(m_hi == s, take(row(ref, c * 3 + n, pl.ds(s, 1)), m_lo), acc)
            nodes.append(acc)
        return ends(nodes, m_is0, m_is1)

    def from_partner(ref, c, f):
        nodes = []
        for n in range(3):
            acc = jnp.zeros(TILE, F32)
            for s in range(8):
                acc = jnp.where(p_loc[f] == s, take(row(ref, c * 3 + n, pl.ds(s, 1)), p_lo[f]), acc)
            nodes.append(acc)
        return ends(nodes, p_is0[f], p_is1[f])

    def from_diag(ref):
        flat = ref.reshape(48 * 8, 128)
        halves = []
        for h in range(2):
            nodes = []
            for n in range(3):
                acc = jnp.zeros(TILE, F32)
                for s in range(8):
                    rows = flat[pl.ds((h * 24 + n) * 8 + s, 8, stride=24), :]
                    acc = jnp.where(d_hi == s, take(rows, d_lo), acc)
                nodes.append(acc)
            halves.append(ends(nodes, d_is0, d_is1))
        return halves

    for f in range(3):
        aux[FACE_NODES[f][0]] = edge[f]
        aux[3 + f] = half_kappa
    for r in range(6, 48):
        aux[r] = jnp.zeros(TILE, F32)
    for r in range(45, 48):
        tab[r] = zone.astype(F32)
    slot_edge = from_slots(aux, 0)[0]
    slot_kedge = from_slots(aux, 1)[0] * slot_edge
    d_aux = from_diag(aux)[0][0]
    d_edge = jnp.broadcast_to(d_aux[0:1], TILE)
    d_kedge = jnp.broadcast_to(d_aux[1:2], TILE) * d_edge
    d_scale = [jnp.where(sub < 4, d_edge, d_kedge), jnp.where(sub < 6, d_kedge, 1.0)]
    kept_ref = kept
    kedge = [half_kappa * edge[f] for f in range(3)]

    def copies(k):
        group = []
        for i, n in enumerate(MAIN):
            group.append((sbuf.at[k, i], rbuf.at[k, 3 - i], i, 3 - i, at(*STEPS[n])))
        for i, n in enumerate(DIAG):
            group.append((sdiag.at[k], rdiag.at[k, 3 - i], 4 + i, 4 + 3 - i, at(*STEPS[n])))
        return [
            pltpu.make_async_remote_copy(
                src_ref=src, dst_ref=dst, send_sem=send_sem.at[k, a], recv_sem=recv_sem.at[k, b],
                device_id=peer, device_id_type=MESH,
            )
            for src, dst, a, b, peer in group
        ]

    tf = jnp.zeros(TILE, F32)
    tc = jnp.zeros(TILE, F32)
    far_terms = [jnp.zeros(TILE, F32)] * 3
    started = []
    weights = {2: 2.0 / 3.0, 1: 0.25, 0: 1.0}
    for k in (2, 1, 0):
        v = cot if k == 2 else lam.at[k]
        weight = weights[k] * DT
        x = xs.at[k]
        xflat = x.reshape(42 * 8, 128)
        for s in range(8):
            xflat[pl.ds(s, 42, stride=8), :] = states[k, :, s * 128 : (s + 1) * 128].astype(F32)
        squares = []
        for n in range(3):
            squares.append(sum(x[c * 3 + n] * x[c * 3 + n] for c in range(4)))
        q = [squares[a] + squares[b] for a, b in FACE_NODES]
        for f in range(3):
            tab[42 + FACE_NODES[f][0]] = q[f]
        wet_area = wet * area
        for r in range(12):
            tab[r] = wet_area * v[r]
        for r in range(12, 42):
            tab[r] = area * v[r]

        last = ZCOMP if k == 2 else QCOMP
        for c in range(last + 1):
            pair = from_slots(tab, c)
            scale = slot_edge if c < 4 else slot_kedge
            for j in range(2 if c < COMPS else 1):
                value = pair[j] * scale if c < COMPS else pair[j]
                ch = c * 2 + j if c < COMPS else 28 + c - COMPS
                for d in range(4):
                    sbuf[k, d, ch] = value[2 * d : 2 * d + 2]
        halves = from_diag(tab)
        for h in range(2):
            for j in range(2):
                sdiag[k, j, h * 8 : h * 8 + 8] = halves[h][j] * d_scale[h]
        if k == 2:
            pl.semaphore_wait(barrier, len(peers))
        group = copies(k)
        for copy in group:
            copy.start()
        started += group

        if k == 2:
            for f in range(3):
                outer_edge = from_partner(aux, 0, f)[0]
                kept_ref[f] = outer_edge
                kept_ref[3 + f] = from_partner(aux, 1, f)[0] * outer_edge
        for f in range(3):
            for c in range(last + 1):
                pair = from_partner(tab, c, f)
                if c < COMPS:
                    scale = kept_ref[f] if c < 4 else kept_ref[3 + f]
                    local[f, c * 2] = pair[0] * scale
                    local[f, c * 2 + 1] = pair[1] * scale
                else:
                    local[f, 28 + c - COMPS] = pair[0]

        moment = jnp.sqrt(1.0 + (1.0 / 6.0) * sum(x[r] * x[r] for r in range(3, 9)))
        wet_friction = wet * rough_zone * moment
        acc = jnp.zeros(TILE, F32)
        for r in range(3, 9):
            acc = acc + v[r] * x[r]
        tf = tf - weight * (wet * rough * moment) * acc
        inner = [[None] * 8 for _ in range(3)]
        bars = [None] * 12
        for r in range(12):
            bars[r] = sum(vol[b, r] * tab[b] for b in range(12))
            if 3 <= r < 9:
                bars[r] = bars[r] - wet_friction * v[r]
        for f in range(3):
            for a in range(8):
                total = sum(
                    fin[b, a] * tab[(b // 2) * 3 + FACE_NODES[f][b % 2]] for b in range(8)
                )
                r = (a // 2) * 3 + FACE_NODES[f][a % 2]
                bars[r] = bars[r] + edge[f] * total
        own = jnp.zeros(TILE, F32)
        node_edge = [
            sum(kedge[f] for f in range(3) if n in FACE_NODES[f]) for n in range(3)
        ]
        for n in range(3):
            above = v[12 + n] - 0.5 * wet * v[9 + n]
            bars[9 + n] = bars[9 + n] + kappa * above
            own = own + kappa * above * (x[9 + n] - x[12 + n])
            for l in range(10):
                r = 12 + l * 3 + n
                below = v[r + 3] - v[r] if l < 9 else None
                if below is not None:
                    own = own + kappa * below * (x[r] - x[r + 3])
                    flow = kappa * (below - above)
                else:
                    flow = -kappa * above
                face = node_edge[n] * tab[r]
                own = own - face * x[r]
                pre[r] = flow - face
                above = below
        for r in range(12):
            pre[r] = bars[r]
        tc = tc + weight * own

        for copy in group:
            copy.wait_recv()
        for j in range(2):
            for h in range(2):
                acc = rdiag[k, 0, j, h * 8 : h * 8 + 8]
                for d in range(1, 4):
                    acc = jnp.where((lane >> 2) == d, rdiag[k, d, j, h * 8 : h * 8 + 8], acc)
                cdiag[j, h * 8 : h * 8 + 8] = acc

        def beyond(f, ch):
            acc = local[f, ch]
            for s in range(8):
                acc = jnp.where(
                    p_rem[f] == s, take(row(rbuf, k, s // 2, ch, pl.ds(s % 2, 1)), p_lo[f]), acc
                )
            if ch < 28:
                j, c = ch % 2, ch // 2
            else:
                j, c = 0, ch - 28 + COMPS
            return jnp.where(p_rem[f] == 8, take(row(cdiag, j, pl.ds(c, 1)), p_lo[f]), acc)

        for f in range(3):
            if k == 2:
                kept_ref[6 + f] = beyond(f, 29)
            outer_q = beyond(f, 28)
            half_speed = 0.5 * jnp.sqrt(1.0 + 0.03125 * (q[f] + outer_q))
            outer = [beyond(f, a) for a in range(8)]
            for a in range(8):
                r = (a // 2) * 3 + FACE_NODES[f][a % 2]
                total = half_speed * (edge[f] * tab[r] - outer[a])
                for b in range(8):
                    total = total - fout[b, a] * outer[b]
                pre[r] = pre[r] + total
            term = jnp.zeros(TILE, F32)
            for ch in range(8, 28):
                r = 12 + ((ch - 8) // 2) * 3 + FACE_NODES[f][ch % 2]
                value = beyond(f, ch)
                term = term + value * x[r]
                pre[r] = pre[r] + value
            far_terms[f] = far_terms[f] + weight * term

        for r in range(42):
            if k == 2:
                lam[1, r] = (2.0 / 3.0) * (cot[r] + DT * pre[r])
            elif k == 1:
                lam[0, r] = 0.25 * (lam[1, r] + DT * pre[r])
            else:
                out[r] = cot[r] * (1.0 / 3.0) + 0.75 * lam[1, r] + lam[0, r] + DT * pre[r]

    base = 4 * (ix * GY + iy)
    friction_bins = [jnp.zeros(TILE, F32) for _ in range(WINDOW // 8)]
    conduct_bins = [jnp.zeros(TILE, F32) for _ in range(WINDOW // 8)]
    own_rel = (zone - base + BEHIND + ZONES) & (ZONES - 1)
    far_rel = [(kept_ref[6 + f].astype(jnp.int32) - base + BEHIND + ZONES) & (ZONES - 1) for f in range(3)]
    for s in range(8):
        rel = jnp.broadcast_to(own_rel[s : s + 1], TILE) - sub
        tf_row = jnp.broadcast_to(tf[s : s + 1], TILE)
        tc_row = jnp.broadcast_to(tc[s : s + 1], TILE)
        for z in (4, 5):
            hit = rel == 8 * z
            friction_bins[z] = friction_bins[z] + jnp.where(hit, tf_row, 0.0)
            conduct_bins[z] = conduct_bins[z] + jnp.where(hit, tc_row, 0.0)
        for f in range(3):
            rel = jnp.broadcast_to(far_rel[f][s : s + 1], TILE) - sub
            term = jnp.broadcast_to(far_terms[f][s : s + 1], TILE)
            for z in range(WINDOW // 8):
                conduct_bins[z] = conduct_bins[z] + jnp.where(rel == 8 * z, term, 0.0)
    ones = jnp.ones(TILE, F32)
    pad = [jnp.zeros(TILE, F32) for _ in range(16 - WINDOW // 8)]

    def lanes(bins):
        return lax.dot_general(
            ones, jnp.concatenate(bins + pad, axis=0), (((1,), (1,)), ((), ())),
            precision=lax.Precision.HIGHEST, preferred_element_type=F32,
        )

    friction_row, conduct_row = lanes(friction_bins), lanes(conduct_bins)
    wide = (sub >> 1) * 128 + lane
    rel = (wide - base + BEHIND + ZONES) & (ZONES - 1)
    spread = jnp.where(
        (sub & 1) == 0, take(friction_row, rel & 127), take(conduct_row, rel & 127)
    )
    spread = jnp.where(rel < WINDOW, spread, 0.0)

    gyb[iy] = spread
    group = [
        pltpu.make_async_remote_copy(
            src_ref=gyb.at[iy], dst_ref=gyb.at[iy], send_sem=gy_send.at[d], recv_sem=gy_recv.at[d],
            device_id=at(0, d), device_id_type=MESH,
        )
        for d in range(1, GY)
    ]
    for copy in group:
        copy.start()
    started += group
    for copy in group:
        copy.wait_recv()
    total = gyb[0]
    for i in range(1, GY):
        total = total + gyb[i]
    gxb[ix] = total
    group = [
        pltpu.make_async_remote_copy(
            src_ref=gxb.at[ix], dst_ref=gxb.at[ix], send_sem=gx_send.at[d], recv_sem=gx_recv.at[d],
            device_id=at(d, 0), device_id_type=MESH,
        )
        for d in range(1, GX)
    ]
    for copy in group:
        copy.start()
    started += group
    for copy in group:
        copy.wait_recv()
    total = gxb[0]
    for i in range(1, GX):
        total = total + gxb[i]
    for t in range(4):
        grads[0:1, t * 128 : (t + 1) * 128] = GRAD_WEIGHT * total[2 * t : 2 * t + 1]
        grads[1:2, t * 128 : (t + 1) * 128] = (
            GRAD_WEIGHT * total[2 * t + 1 : 2 * t + 2] / zc_ref[t : t + 1]
        )
    for copy in started:
        copy.wait_send()


def local(
    cotangent, section_states, inverse_area, edge_length, roughness, soil_conductance, zone_friction,
    zone_conductivity, wet_mask, element_zone, send_face, send_count, face_partner, volume_matrix, flux_in, flux_out,
):
    vmem = pl.BlockSpec(memory_space=pltpu.VMEM)
    smem = pl.BlockSpec(memory_space=pltpu.SMEM)
    adjoint, grads = pl.pallas_call(
        kernel,
        out_shape=(
            jax.ShapeDtypeStruct((42, 8, 128), F32),
            jax.ShapeDtypeStruct((2, ZONES), F32),
        ),
        in_specs=[vmem] * 12 + [smem] * 3,
        out_specs=(vmem, vmem),
        scratch_shapes=[
            pltpu.VMEM((48, 8, 128), F32),
            pltpu.VMEM((48, 8, 128), F32),
            pltpu.VMEM((3, 42, 8, 128), F32),
            pltpu.VMEM((3, 30, 8, 128), F32),
            pltpu.VMEM((42, 8, 128), F32),
            pltpu.VMEM((2, 42, 8, 128), F32),
            pltpu.VMEM((9, 8, 128), F32),
            pltpu.VMEM((3, 4, 30, 2, 128), F32),
            pltpu.VMEM((3, 4, 30, 2, 128), F32),
            pltpu.VMEM((3, 2, 16, 128), F32),
            pltpu.VMEM((3, 4, 2, 16, 128), F32),
            pltpu.VMEM((2, 16, 128), F32),
            pltpu.VMEM((GY, 8, 128), F32),
            pltpu.VMEM((GX, 8, 128), F32),
            pltpu.SemaphoreType.DMA((3, 8)),
            pltpu.SemaphoreType.DMA((3, 8)),
            pltpu.SemaphoreType.DMA((GY,)),
            pltpu.SemaphoreType.DMA((GY,)),
            pltpu.SemaphoreType.DMA((GX,)),
            pltpu.SemaphoreType.DMA((GX,)),
        ],
        compiler_params=pltpu.CompilerParams(
            collective_id=0, has_side_effects=True, vmem_limit_bytes=32 << 20
        ),
        name="sections",
    )(
        cotangent.reshape(42, 8, 128),
        section_states.reshape(3, 42, 1024),
        inverse_area.reshape(8, 128),
        edge_length.reshape(3, 8, 128),
        roughness.reshape(8, 128),
        soil_conductance.reshape(8, 128),
        zone_friction.reshape(4, 128),
        zone_conductivity.reshape(4, 128),
        wet_mask.reshape(8, 128),
        element_zone.reshape(8, 128),
        send_face.reshape(8, 256),
        face_partner.reshape(3, 8, 128),
        volume_matrix,
        flux_in,
        flux_out,
    )
    return adjoint.reshape(1, 1, 42, 1024), grads


def solution(mesh):
    placed = (
        P("gx", "gy", None, None),
        P(None, "gx", "gy", None, None),
        P("gx", "gy", None),
        P("gx", "gy", None, None),
        P("gx", "gy", None),
        P("gx", "gy", None),
        P(),
        P(),
        P("gx", "gy", None),
        P("gx", "gy", None),
        P("gx", "gy", None, None),
        P("gx", "gy", None),
        P("gx", "gy", None, None),
        P(),
        P(),
        P(),
    )
    return jax.shard_map(
        local,
        mesh=mesh,
        in_specs=placed,
        out_specs=(P("gx", "gy", None, None), P()),
        check_vma=False,
    )
```

time: 654 us -> 49.9 us (0.08)
  the two profiles are of different devices: /device:TPU:33 before, /device:TPU:1 now
where the time goes in v1:
time: 49.9 us; the launch traced here: 49.3 us
  Pallas kernels  37.9 us (76%)
  local copies, waits for them, and re-layouts  10.7 us (21%)
  between operations  0.68 us (1%)
    pallas_call x1, Pallas kernels, local(): pl.pallas_call(kernel, out_shape=(jax.ShapeDtypeStruct((42, 8, 128), F32)...  37.9 us
    unnamed x32, local copies, waits for them, and re-layouts  10.7 us

profile of v1, /device:TPU:1, one launch (start us, length us, event | category | flops | bytes accessed | tf_op | source)
XLA Modules:
  0.0 49.3 jit_solution(14393179329556460739)
XLA Ops:
  0.6 0.0 copy-start.2
  0.6 0.0 copy-start.4
  0.7 0.0 copy-start.13
  0.7 0.7 %copy-done.2 = f32[1,1,3,1024]{3,1,2,0:T(1,128)S(1)} copy-done((f32[1,1,3,1024]{3,1,2,0:T(1,128)S(1)}, f32[1,1,3,1024]{3,1,2,0:T(1,128)}, u32[]{:S(2)}) %copy-start.2) | copy-done | bytes 12312
  1.3 0.0 copy-done.4
  1.4 0.0 copy-done.13
  1.4 0.0 copy-start
  1.4 1.0 %copy-done = bf16[3,1,1,42,1024]{4,3,2,1,0:T(8,128)(2,1)S(1)} copy-done((bf16[3,1,1,42,1024]{4,3,2,1,0:T(8,128)(2,1)S(1)}, bf16[3,1,1,42,1024]{4,3,2,1,0:T(8,128)(2,1)}, u32[]{:S(2)}) %copy-start) | copy-done | bytes 258072
  2.3 0.0 copy-start.1
  2.3 0.9 %copy-done.1 = f32[1,1,42,1024]{3,1,2,0:T(1,128)S(1)} copy-done((f32[1,1,42,1024]{3,1,2,0:T(1,128)S(1)}, f32[1,1,42,1024]{3,1,2,0:T(1,128)}, u32[]{:S(2)}) %copy-start.1) | copy-done | bytes 172056
  3.2 0.0 copy-start.3
  3.2 0.7 %copy-done.3 = s32[1,1,3,1024]{3,1,2,0:T(1,128)S(1)} copy-done((s32[1,1,3,1024]{3,1,2,0:T(1,128)S(1)}, s32[1,1,3,1024]{3,1,2,0:T(1,128)}, u32[]{:S(2)}) %copy-start.3) | copy-done | bytes 12312
  3.9 0.0 copy-start.5
  4.0 0.7 %copy-done.5 = f32[12,12]{1,0:T(8,128)S(1)} copy-done((f32[12,12]{1,0:T(8,128)S(1)}, f32[12,12]{1,0:T(8,128)}, u32[]{:S(2)}) %copy-start.5) | copy-done | bytes 600
  4.6 0.0 copy-start.6
  4.6 0.7 %copy-done.6 = f32[1,1,1024]{2,1,0:T(1,128)S(1)} copy-done((f32[1,1,1024]{2,1,0:T(1,128)S(1)}, f32[1,1,1024]{2,1,0:T(1,128)}, u32[]{:S(2)}) %copy-start.6) | copy-done | bytes 4120
  5.3 0.0 copy-start.7
  5.3 0.7 %copy-done.7 = f32[1,1,1024]{2,1,0:T(1,128)S(1)} copy-done((f32[1,1,1024]{2,1,0:T(1,128)S(1)}, f32[1,1,1024]{2,1,0:T(1,128)}, u32[]{:S(2)}) %copy-start.7) | copy-done | bytes 4120
  6.0 0.0 copy-start.8
  6.0 0.7 %copy-done.8 = f32[1,1,1024]{2,1,0:T(1,128)S(1)} copy-done((f32[1,1,1024]{2,1,0:T(1,128)S(1)}, f32[1,1,1024]{2,1,0:T(1,128)}, u32[]{:S(2)}) %copy-start.8) | copy-done | bytes 4120
  6.7 0.0 copy-start.9
  6.7 0.7 %copy-done.9 = s32[1,1,1024]{2,1,0:T(1,128)S(1)} copy-done((s32[1,1,1024]{2,1,0:T(1,128)S(1)}, s32[1,1,1024]{2,1,0:T(1,128)}, u32[]{:S(2)}) %copy-start.9) | copy-done | bytes 4120
  7.4 0.0 copy-start.10
  7.4 0.7 %copy-done.10 = s32[1,1,1024]{2,1,0:T(1,128)S(1)} copy-done((s32[1,1,1024]{2,1,0:T(1,128)S(1)}, s32[1,1,1024]{2,1,0:T(1,128)}, u32[]{:S(2)}) %copy-start.10) | copy-done | bytes 4120
  8.1 0.0 copy-start.11
  8.1 0.7 %copy-done.11 = f32[8,8]{1,0:T(8,128)S(1)} copy-done((f32[8,8]{1,0:T(8,128)S(1)}, f32[8,8]{1,0:T(8,128)}, u32[]{:S(2)}) %copy-start.11) | copy-done | bytes 280
  8.8 0.0 copy-start.12
  8.8 0.7 %copy-done.12 = f32[8,8]{1,0:T(8,128)S(1)} copy-done((f32[8,8]{1,0:T(8,128)S(1)}, f32[8,8]{1,0:T(8,128)}, u32[]{:S(2)}) %copy-start.12) | copy-done | bytes 280
  9.5 0.0 copy-start.14
  9.5 0.7 %copy-done.14 = f32[512]{0:T(512)S(1)} copy-done((f32[512]{0:T(512)S(1)}, f32[512]{0:T(512)}, u32[]{:S(2)}) %copy-start.14) | copy-done | bytes 2072
  10.1 37.9 %sections.1 = (f32[42,8,128]{2,1,0:T(8,128)S(1)}, f32[2,512]{1,0:T(2,128)S(1)}) custom-call(f32[42,8,128]{2,1,0:T(8,128)S(1)} %bitcast.14, bf16[3,42,1024]{2,1,0:T(8,128)(2,1)S(1)} %bitcast.13, f32[8,128]{1,0:T(8,128)S(1)} %bitcast.19, f32[3,8,128]{2,1,0:T(8,128)S(1)} %bitcast.16, f32[8,128]{1,0:T(8,128)S(1)} %bitcast.20, f32[8,128]{1,0:T(8,128)S(1)} %bitcast.21, ...), custom_call_target="tpu_custom_call" | custom-call | tf_op jit(solution)/shard_map/sections/pallas_call | solution.py:407
  48.1 0.7 %copy.21 = f32[1,1,42,1024]{3,1,2,0:T(1,128)} copy(f32[1,1,42,1024]{3,1,2,0:T(1,128)S(1)} %bitcast.15) | data formatting | bytes 344064
  48.7 0.6 %copy.22 = f32[2,512]{1,0:T(2,128)} copy(f32[2,512]{1,0:T(2,128)S(1)} %get-tuple-element.13) | data formatting | bytes 8192
Async XLA Ops:
  0.6 0.7 %copy-start.2 = (f32[1,1,3,1024]{3,1,2,0:T(1,128)S(1)}, f32[1,1,3,1024]{3,1,2,0:T(1,128)}, u32[]{:S(2)}) copy-start(f32[1,1,3,1024]{3,1,2,0:T(1,128)} %param.19) | copy-start | bytes 36868
  0.6 0.7 %copy-start.4 = (s32[1,1,8,256]{3,2,1,0:T(8,128)S(1)}, s32[1,1,8,256]{3,2,1,0:T(8,128)}, u32[]{:S(2)}) copy-start(s32[1,1,8,256]{3,2,1,0:T(8,128)} %param.26) | copy-start | bytes 24580
  0.7 0.7 %copy-start.13 = (f32[512]{0:T(512)S(1)}, f32[512]{0:T(512)}, u32[]{:S(2)}) copy-start(f32[512]{0:T(512)} %param.22) | copy-start | bytes 6148
  1.4 1.0 %copy-start = (bf16[3,1,1,42,1024]{4,3,2,1,0:T(8,128)(2,1)S(1)}, bf16[3,1,1,42,1024]{4,3,2,1,0:T(8,128)(2,1)}, u32[]{:S(2)}) copy-start(bf16[3,1,1,42,1024]{4,3,2,1,0:T(8,128)(2,1)} %param.17) | copy-start | bytes 774148
  2.3 0.9 %copy-start.1 = (f32[1,1,42,1024]{3,1,2,0:T(1,128)S(1)}, f32[1,1,42,1024]{3,1,2,0:T(1,128)}, u32[]{:S(2)}) copy-start(f32[1,1,42,1024]{3,1,2,0:T(1,128)} %param.16) | copy-start | bytes 516100
  3.2 0.7 %copy-start.3 = (s32[1,1,3,1024]{3,1,2,0:T(1,128)S(1)}, s32[1,1,3,1024]{3,1,2,0:T(1,128)}, u32[]{:S(2)}) copy-start(s32[1,1,3,1024]{3,1,2,0:T(1,128)} %param.27) | copy-start | bytes 36868
  3.9 0.7 %copy-start.5 = (f32[12,12]{1,0:T(8,128)S(1)}, f32[12,12]{1,0:T(8,128)}, u32[]{:S(2)}) copy-start(f32[12,12]{1,0:T(8,128)} %vol.1) | copy-start | bytes 1732
  4.6 0.7 %copy-start.6 = (f32[1,1,1024]{2,1,0:T(1,128)S(1)}, f32[1,1,1024]{2,1,0:T(1,128)}, u32[]{:S(2)}) copy-start(f32[1,1,1024]{2,1,0:T(1,128)} %param.18) | copy-start | bytes 12292
  5.3 0.7 %copy-start.7 = (f32[1,1,1024]{2,1,0:T(1,128)S(1)}, f32[1,1,1024]{2,1,0:T(1,128)}, u32[]{:S(2)}) copy-start(f32[1,1,1024]{2,1,0:T(1,128)} %param.20) | copy-start | bytes 12292
  6.0 0.7 %copy-start.8 = (f32[1,1,1024]{2,1,0:T(1,128)S(1)}, f32[1,1,1024]{2,1,0:T(1,128)}, u32[]{:S(2)}) copy-start(f32[1,1,1024]{2,1,0:T(1,128)} %param.21) | copy-start | bytes 12292
  6.7 0.7 %copy-start.9 = (s32[1,1,1024]{2,1,0:T(1,128)S(1)}, s32[1,1,1024]{2,1,0:T(1,128)}, u32[]{:S(2)}) copy-start(s32[1,1,1024]{2,1,0:T(1,128)} %param.24) | copy-start | bytes 12292
  7.4 0.7 %copy-start.10 = (s32[1,1,1024]{2,1,0:T(1,128)S(1)}, s32[1,1,1024]{2,1,0:T(1,128)}, u32[]{:S(2)}) copy-start(s32[1,1,1024]{2,1,0:T(1,128)} %param.25) | copy-start | bytes 12292
  8.1 0.7 %copy-start.11 = (f32[8,8]{1,0:T(8,128)S(1)}, f32[8,8]{1,0:T(8,128)}, u32[]{:S(2)}) copy-start(f32[8,8]{1,0:T(8,128)} %fin.1) | copy-start | bytes 772
  8.8 0.7 %copy-start.12 = (f32[8,8]{1,0:T(8,128)S(1)}, f32[8,8]{1,0:T(8,128)}, u32[]{:S(2)}) copy-start(f32[8,8]{1,0:T(8,128)} %fout.1) | copy-start | bytes 772
  9.5 0.7 %copy-start.14 = (f32[512]{0:T(512)S(1)}, f32[512]{0:T(512)}, u32[]{:S(2)}) copy-start(f32[512]{0:T(512)} %param.23) | copy-start | bytes 6148

commit v2 on v1

v2 whole, which is shorter than its diff:
```python
import jax
import jax.numpy as jnp
from jax import lax
from jax.experimental import pallas as pl
from jax.experimental.pallas import tpu as pltpu
from jax.sharding import PartitionSpec as P

GX, GY = 16, 8
COMPS = 14
QCOMP, ZCOMP = 14, 15
ZONES = 512
DT = 0.2
GRAD_WEIGHT = 1.0 / 64.0
FACE_NODES = ((1, 2), (2, 0), (0, 1))
MAIN = (1, 3, 4, 6)
DIAG = (0, 2, 5, 7)
STEPS = ((-1, -1), (-1, 0), (-1, 1), (0, -1), (0, 1), (1, -1), (1, 0), (1, 1))
WINDOW, BEHIND = 80, 36
MESH = pl.DeviceIdType.MESH
TILE = (8, 128)
F32 = jnp.float32


LOOKUP = lax.GatherDimensionNumbers(
    offset_dims=(), collapsed_slice_dims=(1,), start_index_map=(1,), operand_batching_dims=(0,),
    start_indices_batching_dims=(0,),
)


def lanes_of(idx):
    return idx.reshape(8, 128, 1)


def take(x, idx):
    return lax.gather(
        x, idx, LOOKUP, slice_sizes=(1, 1), mode=lax.GatherScatterMode.PROMISE_IN_BOUNDS
    )


def row(ref, *at):
    return jnp.broadcast_to(ref[at], TILE)


def pick(code, values, like):
    out = jnp.full(TILE, values[-1], like.dtype)
    for i in range(len(values) - 2, -1, -1):
        out = jnp.where(code == i, values[i], out)
    return out


def ends(nodes, is0, is1):
    a, b, c = nodes
    first = lax.select(is0, b, lax.select(is1, c, a))
    second = lax.select(is0, c, lax.select(is1, a, b))
    return first, second


def kernel(
    cot_hbm, states_hbm, area_hbm, edge_hbm, rough_hbm, soil_hbm, zf_hbm, zc_hbm, wet_hbm, zone_hbm, send_hbm,
    partner_hbm, vol_hbm, fin_hbm, fout_hbm,
    out, grads,
    cot, states, area_ref, edge_ref, rough_ref, soil_ref, zf_ref, zc_ref, wet_ref, zone_ref, send_ref, partner_ref,
    vol_ref, fin_ref, fout_ref, vol, fin, fout,
    tab, aux, xs, local, fwd, pre, lam, kept, sbuf, rbuf, sdiag, rdiag, cdiag, gyb, gxb,
    in_sem, send_sem, recv_sem, gy_send, gy_recv, gx_send, gx_recv,
):
    ix, iy = lax.axis_index("gx"), lax.axis_index("gy")

    def at(dx, dy):
        return (lax.rem(ix + dx + GX, GX), lax.rem(iy + dy + GY, GY))

    side_x = {-1: (ix + GX - 1) // GX, 0: 1, 1: (2 * GX - 2 - ix) // GX}
    side_y = {-1: (iy + GY - 1) // GY, 0: 1, 1: (2 * GY - 2 - iy) // GY}

    def exists(n):
        dx, dy = STEPS[n]
        return side_x[dx] * side_y[dy] == 1

    barrier = pltpu.get_barrier_semaphore()
    peers = [at(0, k) for k in range(1, GY)] + [at(k, 0) for k in range(1, GX)]
    for n in DIAG:
        @pl.when(exists(n))
        def _():
            pl.semaphore_signal(barrier, inc=1, device_id=at(*STEPS[n]), device_id_type=MESH)
    for peer in reversed(peers):
        pl.semaphore_signal(barrier, inc=1, device_id=peer, device_id_type=MESH)
    greeters = len(peers) + (side_x[-1] + side_x[1]) * (side_y[-1] + side_y[1])

    inputs = (
        (cot_hbm, cot), (states_hbm, states), (area_hbm, area_ref), (edge_hbm, edge_ref), (rough_hbm, rough_ref),
        (soil_hbm, soil_ref), (zf_hbm, zf_ref), (zc_hbm, zc_ref), (wet_hbm, wet_ref), (zone_hbm, zone_ref),
        (send_hbm, send_ref), (partner_hbm, partner_ref), (vol_hbm, vol_ref), (fin_hbm, fin_ref), (fout_hbm, fout_ref),
    )
    reads = [pltpu.make_async_copy(src, dst, in_sem.at[i]) for i, (src, dst) in enumerate(inputs)]
    for read in reads:
        read.start()
    for read in reads:
        read.wait()

    sub = lax.broadcasted_iota(jnp.int32, TILE, 0)
    lane = lax.broadcasted_iota(jnp.int32, TILE, 1)

    area = area_ref[...]
    rough = rough_ref[...]
    wet = wet_ref[...].astype(F32)
    zone = zone_ref[...]
    edge = [edge_ref[f] for f in range(3)]
    kappa = jnp.zeros(TILE, F32)
    zfric = jnp.zeros(TILE, F32)
    zlane, zhi = lanes_of(zone & 127), zone >> 7
    for t in range(4):
        kappa = jnp.where(zhi == t, take(row(zc_ref, pl.ds(t, 1)), zlane), kappa)
        zfric = jnp.where(zhi == t, take(row(zf_ref, pl.ds(t, 1)), zlane), zfric)
    kappa = kappa * soil_ref[...]
    half_kappa = 0.5 * kappa
    rough_zone = zfric * rough

    slots = jnp.concatenate(
        [send_ref[n : n + 1, h * 128 : (h + 1) * 128] for n in MAIN for h in range(2)], axis=0
    )
    m_lo, m_f = lanes_of(slots & 127), slots >> 10
    m_hi = [((slots >> 7) & 7) == t for t in range(8)]
    m_is0, m_is1 = m_f == 0, m_f == 1
    dslots = jnp.zeros(TILE, jnp.int32)
    for i, n in enumerate(DIAG):
        first = jnp.broadcast_to(send_ref[n : n + 1, 0:128], TILE)
        d = 3 - i
        moved = pltpu.roll(first, 4 * d, axis=1) if d else first
        dslots = jnp.where((lane >> 2) == d, moved, dslots)
    d_lo, d_f = lanes_of(dslots & 127), dslots >> 10
    d_hi = [((dslots >> 7) & 7) == t for t in range(8)]
    d_is0, d_is1 = d_f == 0, d_f == 1

    p_lo, p_loc, p_rem, p_is0, p_is1 = [], [], [], [], []
    for f in range(3):
        p = partner_ref[f]
        there = p - 3072
        n = there >> 8
        slot_row = pick(n, (8, 0, 8, 2, 4, 8, 6, 8), p) + ((there >> 7) & 1)
        is_diag = (n == 0) | (n == 2) | (n == 5) | (n == 7)
        far = p >= 3072
        d_lane = pick(n, (0, 0, 4, 0, 0, 8, 0, 12), p) + (p & 3)
        p_lo.append(lanes_of(jnp.where(far & is_diag, d_lane, p & 127)))
        chunk = jnp.where(far, -1, (p >> 7) & 7)
        p_loc.append([chunk == t for t in range(8)])
        chunk = jnp.where(far, jnp.where(is_diag, 8, slot_row), -1)
        p_rem.append([chunk == t for t in range(9)])
        p_is0.append((p >> 10) == 0)
        p_is1.append((p >> 10) == 1)

    def from_slots(ref, c):
        nodes = []
        for n in range(3):
            acc = jnp.zeros(TILE, F32)
            for s in range(8):
                acc = lax.select(m_hi[s], take(row(ref, c * 3 + n, pl.ds(s, 1)), m_lo), acc)
            nodes.append(acc)
        return ends(nodes, m_is0, m_is1)

    def from_partner(ref, c, f):
        nodes = []
        for n in range(3):
            acc = jnp.zeros(TILE, F32)
            for s in range(8):
                acc = lax.select(p_loc[f][s], take(row(ref, c * 3 + n, pl.ds(s, 1)), p_lo[f]), acc)
            nodes.append(acc)
        return ends(nodes, p_is0[f], p_is1[f])

    def from_diag(ref, first, count):
        rows = ref.shape[0]
        flat = ref.reshape(rows * 8, 128)
        parts = []
        for h in range(count):
            nodes = []
            for n in range(3):
                acc = jnp.zeros(TILE, F32)
                for s in range(8):
                    got = flat[pl.ds(((first + h * 8) * 3 + n) * 8 + s, 8, stride=24), :]
                    acc = lax.select(d_hi[s], take(got, d_lo), acc)
                nodes.append(acc)
            parts.append(ends(nodes, d_is0, d_is1))
        return parts

    for small, wide, size in ((vol_ref, vol, 12), (fin_ref, fin, 8), (fout_ref, fout, 8)):
        for b in range(size):
            for a in range(size):
                wide[b * size + a] = jnp.broadcast_to(small[b : b + 1, a : a + 1], TILE)

    for f in range(3):
        aux[FACE_NODES[f][0]] = edge[f]
        aux[3 + f] = half_kappa
    for r in range(6, 24):
        aux[r] = jnp.zeros(TILE, F32)
    for r in range(45, 48):
        tab[r] = zone.astype(F32)
    slot_edge = from_slots(aux, 0)[0]
    slot_kedge = from_slots(aux, 1)[0] * slot_edge
    d_aux = from_diag(aux, 0, 1)[0][0]
    d_edge = jnp.broadcast_to(d_aux[0:1], TILE)
    d_kedge = jnp.broadcast_to(d_aux[1:2], TILE) * d_edge
    d_scale = [jnp.where(sub < 4, d_edge, d_kedge), jnp.where(sub < 6, d_kedge, 1.0)]
    kedge = [half_kappa * edge[f] for f in range(3)]

    sends = []

    def remote(src, dst, ssem, rsem, n):
        return pltpu.make_async_remote_copy(
            src_ref=src, dst_ref=dst, send_sem=ssem, recv_sem=rsem, device_id=at(*STEPS[n]), device_id_type=MESH
        )

    def main_copy(k, i):
        return remote(
            sbuf.at[k, i], rbuf.at[k, 3 - i], send_sem.at[k, i], recv_sem.at[k, 3 - i], MAIN[i]
        )

    def diag_copy(k, i):
        return remote(
            sdiag.at[k], rdiag.at[k, 3 - i], send_sem.at[k, 4 + i], recv_sem.at[k, 7 - i], DIAG[i]
        )

    def send(make, k, table, order):
        for i in order:
            @pl.when(exists(table[i]))
            def _():
                make(k, i).start()
            sends.append((make, k, table, i))

    def arrive(make, k, table, which):
        for i in which:
            @pl.when(exists(table[i]))
            def _():
                make(k, 3 - i).wait_recv()

    def send_slots(k, ref, comps, first_channel, scales):
        for c in comps:
            pair = from_slots(ref, c)
            for j in range(2 if c < COMPS else 1):
                value = pair[j] * scales(c) if c < COMPS and scales else pair[j]
                ch = c * 2 + j - first_channel if c < COMPS else 28 + c - COMPS
                for d in range(4):
                    sbuf[k, d, ch] = value[2 * d : 2 * d + 2]
        send(main_copy, k, MAIN, (0, 3, 1, 2))

    def merge_diag(k):
        for j in range(2):
            for h in range(2):
                acc = rdiag[k, 0, j, h * 8 : h * 8 + 8]
                for d in range(1, 4):
                    acc = jnp.where((lane >> 2) == d, rdiag[k, d, j, h * 8 : h * 8 + 8], acc)
                cdiag[k, j, h * 8 : h * 8 + 8] = acc

    def receive(k, ref, channels, rows):
        for f in range(3):
            for ch in channels:
                acc = ref[f, ch]
                for s in rows:
                    acc = lax.select(
                        p_rem[f][s], take(row(rbuf, k, s // 2, ch, pl.ds(s % 2, 1)), p_lo[f]), acc
                    )
                ref[f, ch] = acc

    def receive_diag(k, ref, f, ch, c, j):
        return lax.select(p_rem[f][8], take(row(cdiag, k, j, pl.ds(c, 1)), p_lo[f]), ref[f, ch])

    base = 4 * (ix * GY + iy)

    def relative(ids):
        return (ids - base + (BEHIND + ZONES)) & (ZONES - 1)

    tf = jnp.zeros(TILE, F32)
    tc = jnp.zeros(TILE, F32)
    far_terms = [jnp.zeros(TILE, F32)] * 3
    weights = {2: 2.0 / 3.0, 1: 0.25, 0: 1.0}
    FWD = 3

    def own_terms(k, v, x, weight, tf, tc):
        moment = jnp.sqrt(1.0 + (1.0 / 6.0) * sum(x[r] * x[r] for r in range(3, 9)))
        acc = jnp.zeros(TILE, F32)
        for r in range(3, 9):
            acc = acc + v[r] * x[r]
        tf = tf - weight * (wet * rough * moment) * acc
        flows = jnp.zeros(TILE, F32)
        faces = jnp.zeros(TILE, F32)
        for n in range(3):
            above = v[12 + n] - 0.5 * wet * v[9 + n]
            flows = flows + above * (x[9 + n] - x[12 + n])
            acc = tab[12 + n] * x[12 + n]
            for l in range(10):
                r = 12 + l * 3 + n
                if l:
                    acc = acc + tab[r] * x[r]
                if l < 9:
                    flows = flows + (v[r + 3] - v[r]) * (x[r] - x[r + 3])
            faces = faces + sum(kedge[f] for f in range(3) if n in FACE_NODES[f]) * acc
        tc = tc + weight * (kappa * flows - faces)
        return tf, tc, wet * rough_zone * moment

    def zone_bins(tf, tc):
        bins_f = [jnp.zeros(TILE, F32) for _ in range(WINDOW // 8)]
        bins_c = [jnp.zeros(TILE, F32) for _ in range(WINDOW // 8)]
        none = jnp.zeros(TILE, F32)
        own_rel = relative(zone)
        far_rel = [relative(kept[6 + f].astype(jnp.int32)) for f in range(3)]
        for s in range(8):
            rel = jnp.broadcast_to(own_rel[s : s + 1], TILE) - sub
            tf_row = jnp.broadcast_to(tf[s : s + 1], TILE)
            tc_row = jnp.broadcast_to(tc[s : s + 1], TILE)
            for z in (4, 5):
                hit = rel == 8 * z
                bins_f[z] = bins_f[z] + lax.select(hit, tf_row, none)
                bins_c[z] = bins_c[z] + lax.select(hit, tc_row, none)
            for f in range(3):
                rel = jnp.broadcast_to(far_rel[f][s : s + 1], TILE) - sub
                term = jnp.broadcast_to(far_terms[f][s : s + 1], TILE)
                for z in range(WINDOW // 8):
                    bins_c[z] = bins_c[z] + lax.select(rel == 8 * z, term, none)
        ones = jnp.ones(TILE, F32)
        pad = [jnp.zeros(TILE, F32) for _ in range(16 - WINDOW // 8)]

        def lanes(bins):
            return lax.dot_general(
                ones, jnp.concatenate(bins + pad, axis=0), (((1,), (1,)), ((), ())),
                precision=lax.Precision.HIGHEST, preferred_element_type=F32,
            )

        friction_row, conduct_row = lanes(bins_f), lanes(bins_c)
        rel = relative((sub >> 1) * 128 + lane)
        at_rel = lanes_of(rel & 127)
        spread = jnp.where(
            (sub & 1) == 0, take(friction_row, at_rel), take(conduct_row, at_rel)
        )
        return jnp.where(rel < WINDOW, spread, 0.0)

    gy_copies = [
        pltpu.make_async_remote_copy(
            src_ref=gyb.at[iy], dst_ref=gyb.at[iy], send_sem=gy_send.at[d], recv_sem=gy_recv.at[d],
            device_id=at(0, d), device_id_type=MESH,
        )
        for d in (4, 3, 5, 2, 6, 1, 7)
    ]
    gx_copies = [
        pltpu.make_async_remote_copy(
            src_ref=gxb.at[ix], dst_ref=gxb.at[ix], send_sem=gx_send.at[d], recv_sem=gx_recv.at[d],
            device_id=at(d, 0), device_id_type=MESH,
        )
        for d in (8, 6, 10, 7, 9, 5, 11, 4, 12, 3, 13, 2, 14, 1, 15)
    ]

    for k in (2, 1, 0):
        v = cot if k == 2 else lam.at[k]
        weight = weights[k] * DT
        x = xs.at[k]
        if k == 2:
            for m in (2, 0, 1):
                xflat = xs.at[m].reshape(42 * 8, 128)
                for s in range(8):
                    xflat[pl.ds(s, 42, stride=8), :] = states[m, :, s * 128 : (s + 1) * 128].astype(F32)
        squares = []
        for n in range(3):
            squares.append(sum(x[c * 3 + n] * x[c * 3 + n] for c in range(4)))
        q = [squares[a] + squares[b] for a, b in FACE_NODES]
        for f in range(3):
            tab[42 + FACE_NODES[f][0]] = q[f]
        wet_area = wet * area
        for r in range(12):
            tab[r] = wet_area * v[r]
        for r in range(12, 42):
            tab[r] = area * v[r]

        if k == 0:
            tf, tc, wet_friction = own_terms(k, v, x, weight, tf, tc)
            for f in range(3):
                term = jnp.zeros(TILE, F32)
                for ch in range(8, 28):
                    r = 12 + ((ch - 8) // 2) * 3 + FACE_NODES[f][ch % 2]
                    term = term + fwd[f, ch - 8] * tab[r]
                tc = tc + weight * kedge[f] * term
            gyb[iy] = zone_bins(tf, tc)
            for copy in gy_copies:
                copy.start()

        last = ZCOMP if k == 2 else QCOMP
        halves = from_diag(tab, 0, 2)
        for h in range(2):
            for j in range(2):
                sdiag[k, j, h * 8 : h * 8 + 8] = halves[h][j] * d_scale[h]
        if k == 2:
            pl.semaphore_wait(barrier, greeters)
        send(diag_copy, k, DIAG, (0, 1, 2, 3))
        send_slots(k, tab, range(last + 1), 0, lambda c: slot_edge if c < 4 else slot_kedge)

        if k == 2:
            for f in range(3):
                outer_edge = from_partner(aux, 0, f)[0]
                kept[f] = outer_edge
                kept[3 + f] = from_partner(aux, 1, f)[0] * outer_edge
        for f in range(3):
            for c in range(last + 1):
                pair = from_partner(tab, c, f)
                if c < COMPS:
                    scale = kept[f] if c < 4 else kept[3 + f]
                    local[f, c * 2] = pair[0] * scale
                    local[f, c * 2 + 1] = pair[1] * scale
                else:
                    local[f, 28 + c - COMPS] = pair[0]

        if k > 0:
            tf, tc, wet_friction = own_terms(k, v, x, weight, tf, tc)
        bars = [None] * 12
        for r in range(12):
            bars[r] = sum(vol[b * 12 + r] * tab[b] for b in range(12))
            if 3 <= r < 9:
                bars[r] = bars[r] - wet_friction * v[r]
        for f in range(3):
            for a in range(8):
                total = sum(
                    fin[b * 8 + a] * tab[(b // 2) * 3 + FACE_NODES[f][b % 2]] for b in range(8)
                )
                r = (a // 2) * 3 + FACE_NODES[f][a % 2]
                bars[r] = bars[r] + edge[f] * total
        for n in range(3):
            node_edge = sum(kedge[f] for f in range(3) if n in FACE_NODES[f])
            above = v[12 + n] - 0.5 * wet * v[9 + n]
            bars[9 + n] = bars[9 + n] + kappa * above
            for l in range(10):
                r = 12 + l * 3 + n
                below = v[r + 3] - v[r] if l < 9 else 0.0
                pre[r] = kappa * (below - above) - node_edge * tab[r]
                above = below
        for r in range(12):
            pre[r] = bars[r]

        if k == 2:
            halves = from_diag(xs.at[0], 4, 1) + from_diag(xs.at[0], 6, 1)
            for h in range(2):
                for j in range(2):
                    sdiag[FWD, j, h * 8 : h * 8 + 8] = halves[h][j]
            send(diag_copy, FWD, DIAG, (0, 1, 2, 3))
            send_slots(FWD, xs.at[0], range(4, COMPS), 8, None)
        if k == 1:
            for f in range(3):
                for c in range(4, COMPS):
                    pair = from_partner(xs.at[0], c, f)
                    fwd[f, c * 2 - 8] = pair[0]
                    fwd[f, c * 2 - 7] = pair[1]
            arrive(main_copy, FWD, MAIN, range(4))
            arrive(diag_copy, FWD, DIAG, range(4))
            merge_diag(FWD)
            receive(FWD, fwd, range(20), range(8))
            for f in range(3):
                for ch in range(20):
                    c = ch // 2 if ch < 4 else ch // 2 + 6
                    fwd[f, ch] = receive_diag(FWD, fwd, f, ch, c, ch % 2)
        if k == 0:
            for copy in gy_copies:
                copy.wait_recv()
            total = gyb[0]
            for i in range(1, GY):
                total = total + gyb[i]
            gxb[ix] = total
            for copy in gx_copies:
                copy.start()

        channels = range(30 if k == 2 else 29)
        arrive(main_copy, k, MAIN, (1, 2))
        receive(k, local, channels, range(2, 6))
        arrive(main_copy, k, MAIN, (0, 3))
        receive(k, local, channels, (0, 1, 6, 7))
        arrive(diag_copy, k, DIAG, range(4))
        merge_diag(k)
        for f in range(3):
            if k == 2:
                kept[6 + f] = receive_diag(k, local, f, 29, ZCOMP, 0)
            outer_q = receive_diag(k, local, f, 28, QCOMP, 0)
            half_speed = 0.5 * jnp.sqrt(1.0 + 0.03125 * (q[f] + outer_q))
            outer = [receive_diag(k, local, f, a, a // 2, a % 2) for a in range(8)]
            for a in range(8):
                r = (a // 2) * 3 + FACE_NODES[f][a % 2]
                total = half_speed * (edge[f] * tab[r] - outer[a])
                for b in range(8):
                    total = total - fout[b * 8 + a] * outer[b]
                pre[r] = pre[r] + total
            term = jnp.zeros(TILE, F32)
            for ch in range(8, 28):
                r = 12 + ((ch - 8) // 2) * 3 + FACE_NODES[f][ch % 2]
                value = receive_diag(k, local, f, ch, ch // 2, ch % 2)
                if k > 0:
                    term = term + value * x[r]
                pre[r] = pre[r] + value
            far_terms[f] = far_terms[f] + weight * term

        for r in range(42):
            if k == 2:
                lam[1, r] = (2.0 / 3.0) * (cot[r] + DT * pre[r])
            elif k == 1:
                lam[0, r] = 0.25 * (lam[1, r] + DT * pre[r])
            else:
                out[r] = cot[r] * (1.0 / 3.0) + 0.75 * lam[1, r] + lam[0, r] + DT * pre[r]

    for copy in gx_copies:
        copy.wait_recv()
    total = gxb[0]
    for i in range(1, GX):
        total = total + gxb[i]
    for t in range(4):
        grads[0:1, t * 128 : (t + 1) * 128] = GRAD_WEIGHT * total[2 * t : 2 * t + 1]
        grads[1:2, t * 128 : (t + 1) * 128] = (
            GRAD_WEIGHT * total[2 * t + 1 : 2 * t + 2] / zc_ref[t : t + 1]
        )
    for make, k, table, i in sends:
        @pl.when(exists(table[i]))
        def _():
            make(k, i).wait_send()
    for copy in gy_copies + gx_copies:
        copy.wait_send()


def local(
    cotangent, section_states, inverse_area, edge_length, roughness, soil_conductance, zone_friction,
    zone_conductivity, wet_mask, element_zone, send_face, send_count, face_partner, volume_matrix, flux_in, flux_out,
):
    vmem = pl.BlockSpec(memory_space=pltpu.VMEM)
    adjoint, grads = pl.pallas_call(
        kernel,
        out_shape=(
            jax.ShapeDtypeStruct((42, 8, 128), F32),
            jax.ShapeDtypeStruct((2, ZONES), F32),
        ),
        in_specs=[pl.BlockSpec(memory_space=pl.ANY)] * 15,
        out_specs=(vmem, vmem),
        scratch_shapes=[
            pltpu.VMEM((42, 8, 128), F32),
            pltpu.VMEM((3, 42, 1024), jnp.bfloat16),
            pltpu.VMEM((8, 128), F32),
            pltpu.VMEM((3, 8, 128), F32),
            pltpu.VMEM((8, 128), F32),
            pltpu.VMEM((8, 128), F32),
            pltpu.VMEM((4, 128), F32),
            pltpu.VMEM((4, 128), F32),
            pltpu.VMEM((8, 128), jnp.int32),
            pltpu.VMEM((8, 128), jnp.int32),
            pltpu.VMEM((8, 256), jnp.int32),
            pltpu.VMEM((3, 8, 128), jnp.int32),
            pltpu.VMEM((12, 12), F32),
            pltpu.VMEM((8, 8), F32),
            pltpu.VMEM((8, 8), F32),
            pltpu.VMEM((144, 8, 128), F32),
            pltpu.VMEM((64, 8, 128), F32),
            pltpu.VMEM((64, 8, 128), F32),
            pltpu.VMEM((48, 8, 128), F32),
            pltpu.VMEM((24, 8, 128), F32),
            pltpu.VMEM((3, 42, 8, 128), F32),
            pltpu.VMEM((3, 30, 8, 128), F32),
            pltpu.VMEM((3, 20, 8, 128), F32),
            pltpu.VMEM((42, 8, 128), F32),
            pltpu.VMEM((2, 42, 8, 128), F32),
            pltpu.VMEM((9, 8, 128), F32),
            pltpu.VMEM((4, 4, 30, 2, 128), F32),
            pltpu.VMEM((4, 4, 30, 2, 128), F32),
            pltpu.VMEM((4, 2, 16, 128), F32),
            pltpu.VMEM((4, 4, 2, 16, 128), F32),
            pltpu.VMEM((4, 2, 16, 128), F32),
            pltpu.VMEM((GY, 8, 128), F32),
            pltpu.VMEM((GX, 8, 128), F32),
            pltpu.SemaphoreType.DMA((15,)),
            pltpu.SemaphoreType.DMA((4, 8)),
            pltpu.SemaphoreType.DMA((4, 8)),
            pltpu.SemaphoreType.DMA((GY,)),
            pltpu.SemaphoreType.DMA((GY,)),
            pltpu.SemaphoreType.DMA((GX,)),
            pltpu.SemaphoreType.DMA((GX,)),
        ],
        compiler_params=pltpu.CompilerParams(
            collective_id=0, has_side_effects=True, vmem_limit_bytes=63 << 20
        ),
        name="sections",
    )(
        cotangent.reshape(42, 8, 128),
        section_states.reshape(3, 42, 1024),
        inverse_area.reshape(8, 128),
        edge_length.reshape(3, 8, 128),
        roughness.reshape(8, 128),
        soil_conductance.reshape(8, 128),
        zone_friction.reshape(4, 128),
        zone_conductivity.reshape(4, 128),
        wet_mask.reshape(8, 128),
        element_zone.reshape(8, 128),
        send_face.reshape(8, 256),
        face_partner.reshape(3, 8, 128),
        volume_matrix,
        flux_in,
        flux_out,
    )
    return adjoint.reshape(1, 1, 42, 1024), grads


def solution(mesh):
    placed = (
        P("gx", "gy", None, None),
        P(None, "gx", "gy", None, None),
        P("gx", "gy", None),
        P("gx", "gy", None, None),
        P("gx", "gy", None),
        P("gx", "gy", None),
        P(),
        P(),
        P("gx", "gy", None),
        P("gx", "gy", None),
        P("gx", "gy", None, None),
        P("gx", "gy", None),
        P("gx", "gy", None, None),
        P(),
        P(),
        P(),
    )
    return jax.shard_map(
        local,
        mesh=mesh,
        in_specs=placed,
        out_specs=(P("gx", "gy", None, None), P()),
        check_vma=False,
    )
```

time: 49.9 us -> 31.6 us (0.63)
  Pallas kernels: 37.9 us -> 28.6 us
  local copies, waits for them, and re-layouts: 10.7 us -> 2.2 us
    pallas_call x1, Pallas kernels: 37.9 us -> 28.6 us  [local(): pl.pallas_call(kernel, out_shape=(jax.ShapeDtypeStruct((42, 8, 128), F32)...]
    unnamed x32 -> x4, local copies, waits for them, and re-layouts: 10.7 us -> 2.2 us
where the time goes in v2:
time: 31.6 us; the launch traced here: 31.4 us
  Pallas kernels  28.6 us (91%)
  local copies, waits for them, and re-layouts  2.2 us (7%)
  between operations  0.65 us (2%)
    pallas_call x1, Pallas kernels, local(): pl.pallas_call(kernel, out_shape=(jax.ShapeDtypeStruct((42, 8, 128), F32)...  28.6 us
    unnamed x4, local copies, waits for them, and re-layouts  2.2 us

profile of v2, /device:TPU:1, one launch (start us, length us, event | category | flops | bytes accessed | tf_op | source)
XLA Modules:
  0.0 31.4 jit_solution(9654146573378635866)
XLA Ops:
  0.6 28.6 %sections.1 = (f32[42,8,128]{2,1,0:T(8,128)}, f32[2,512]{1,0:T(2,128)}) custom-call(f32[42,8,128]{2,1,0:T(8,128)} %bitcast.14, bf16[3,42,1024]{2,1,0:T(8,128)(2,1)} %bitcast.13, f32[8,128]{1,0:T(8,128)} %bitcast.19, f32[3,8,128]{2,1,0:T(8,128)} %bitcast.16, f32[8,128]{1,0:T(8,128)} %bitcast.20, f32[8,128]{1,0:T(8,128)} %bitcast.21, f32[4,128]{1,0:T(4,128)} %bitcast.24, ...), custom_call_target="tpu_custom_call" | custom-call | tf_op jit(solution)/shard_map/sections/pallas_call | solution.py:523
  29.2 0.0 copy-start
  29.2 1.6 %copy.21 = f32[1,1,42,1024]{3,1,2,0:T(1,128)} copy(f32[1,1,42,1024]{3,1,2,0:T(1,128)} %bitcast.15) | data formatting | bytes 344064
  30.8 0.0 copy-done
  30.8 0.6 %copy.22 = f32[2,512]{1,0:T(2,128)} copy(f32[2,512]{1,0:T(2,128)S(1)} %copy-done) | data formatting | bytes 8192
Async XLA Ops:
  29.2 1.6 %copy-start = (f32[2,512]{1,0:T(2,128)S(1)}, f32[2,512]{1,0:T(2,128)}, u32[]{:S(2)}) copy-start(f32[2,512]{1,0:T(2,128)} %get-tuple-element.13) | copy-start | bytes 12292

commit v3 on v2

--- a/solution.py
+++ b/solution.py
@@ -11,11 +11,13 @@
 ZONES = 512
 DT = 0.2
 GRAD_WEIGHT = 1.0 / 64.0
+SPLIT = 7
+FIRST = 2 + 2 * SPLIT
 FACE_NODES = ((1, 2), (2, 0), (0, 1))
 MAIN = (1, 3, 4, 6)
 DIAG = (0, 2, 5, 7)
 STEPS = ((-1, -1), (-1, 0), (-1, 1), (0, -1), (0, 1), (1, -1), (1, 0), (1, 1))
-WINDOW, BEHIND = 80, 36
+WINDOW, BEHIND = 88, 40
 MESH = pl.DeviceIdType.MESH
 TILE = (8, 128)
 F32 = jnp.float32
@@ -77,12 +79,14 @@
         return side_x[dx] * side_y[dy] == 1
 
     barrier = pltpu.get_barrier_semaphore()
-    peers = [at(0, k) for k in range(1, GY)] + [at(k, 0) for k in range(1, GX)]
+    peers = [at(k, 0) for k in (1, 15)] + [at(0, k) for k in (1, 7)]
+    peers += [at(k, 0) for k in (8, 7, 9, 6, 10, 5, 11, 4, 12, 3, 13, 2, 14)]
+    peers += [at(0, k) for k in (4, 3, 5, 2, 6)]
     for n in DIAG:
         @pl.when(exists(n))
         def _():
             pl.semaphore_signal(barrier, inc=1, device_id=at(*STEPS[n]), device_id_type=MESH)
-    for peer in reversed(peers):
+    for peer in peers:
         pl.semaphore_signal(barrier, inc=1, device_id=peer, device_id_type=MESH)
     greeters = len(peers) + (side_x[-1] + side_x[1]) * (side_y[-1] + side_y[1])
 
@@ -100,6 +104,8 @@
     sub = lax.broadcasted_iota(jnp.int32, TILE, 0)
     lane = lax.broadcasted_iota(jnp.int32, TILE, 1)
 
+    lane16 = [(lane >> 4) == g for g in range(4)]
+    lane4 = [((lane >> 2) & 3) == d for d in range(4)]
     area = area_ref[...]
     rough = rough_ref[...]
     wet = wet_ref[...].astype(F32)
@@ -181,11 +187,6 @@
             parts.append(ends(nodes, d_is0, d_is1))
         return parts
 
-    for small, wide, size in ((vol_ref, vol, 12), (fin_ref, fin, 8), (fout_ref, fout, 8)):
-        for b in range(size):
-            for a in range(size):
-                wide[b * size + a] = jnp.broadcast_to(small[b : b + 1, a : a + 1], TILE)
-
     for f in range(3):
         aux[FACE_NODES[f][0]] = edge[f]
         aux[3 + f] = half_kappa
@@ -208,10 +209,19 @@
             src_ref=src, dst_ref=dst, send_sem=ssem, recv_sem=rsem, device_id=at(*STEPS[n]), device_id_type=MESH
         )
 
-    def main_copy(k, i):
+    def part_copy(k, i, rows, a):
         return remote(
-            sbuf.at[k, i], rbuf.at[k, 3 - i], send_sem.at[k, i], recv_sem.at[k, 3 - i], MAIN[i]
+            sbuf.at[k, i, rows], rbuf.at[k, 3 - i, rows], send_sem.at[k, a + i], recv_sem.at[k, a + 3 - i], MAIN[i]
         )
+
+    def first_copy(k, i):
+        return part_copy(k, i, pl.ds(0, FIRST), 0)
+
+    def second_copy(k, i):
+        return part_copy(k, i, pl.ds(FIRST, 30 - FIRST), 8)
+
+    def forward_copy(k, i):
+        return part_copy(k, i, pl.ds(0, 20), 0)
 
     def diag_copy(k, i):
         return remote(
@@ -231,23 +241,38 @@
             def _():
                 make(k, 3 - i).wait_recv()
 
-    def send_slots(k, ref, comps, first_channel, scales):
+    def fill_slots(k, ref, comps, first_channel, scales):
         for c in comps:
             pair = from_slots(ref, c)
             for j in range(2 if c < COMPS else 1):
                 value = pair[j] * scales(c) if c < COMPS and scales else pair[j]
-                ch = c * 2 + j - first_channel if c < COMPS else 28 + c - COMPS
+                ch = c * 2 + j + first_channel if c < COMPS else c - COMPS
                 for d in range(4):
                     sbuf[k, d, ch] = value[2 * d : 2 * d + 2]
-        send(main_copy, k, MAIN, (0, 3, 1, 2))
-
-    def merge_diag(k):
+
+    def unpack_state(m):
+        flat = xs.at[m].reshape(42 * 8, 128)
+        for s in range(8):
+            flat[pl.ds(s, 42, stride=8), :] = states[m, :, s * 128 : (s + 1) * 128].astype(F32)
+
+    def pack_diag(k, halves, scales):
+        packed = jnp.zeros(TILE, F32)
         for j in range(2):
             for h in range(2):
-                acc = rdiag[k, 0, j, h * 8 : h * 8 + 8]
-                for d in range(1, 4):
-                    acc = jnp.where((lane >> 2) == d, rdiag[k, d, j, h * 8 : h * 8 + 8], acc)
-                cdiag[k, j, h * 8 : h * 8 + 8] = acc
+                g = 2 * j + h
+                value = halves[h][j] * scales[h] if scales else halves[h][j]
+                packed = lax.select(lane16[g], pltpu.roll(value, 16 * g, axis=1) if g else value, packed)
+        sdiag[k] = packed
+        send(diag_copy, k, DIAG, (0, 1, 2, 3))
+
+    def merge_diag(k):
+        acc = rdiag[k, 0]
+        for d in range(1, 4):
+            acc = lax.select(lane4[d], rdiag[k, d], acc)
+        for j in range(2):
+            for h in range(2):
+                g = 2 * j + h
+                cdiag[k, j, h * 8 : h * 8 + 8] = pltpu.roll(acc, 128 - 16 * g, axis=1) if g else acc
 
     def receive(k, ref, channels, rows):
         for f in range(3):
@@ -305,7 +330,7 @@
             rel = jnp.broadcast_to(own_rel[s : s + 1], TILE) - sub
             tf_row = jnp.broadcast_to(tf[s : s + 1], TILE)
             tc_row = jnp.broadcast_to(tc[s : s + 1], TILE)
-            for z in (4, 5):
+            for z in (5,):
                 hit = rel == 8 * z
                 bins_f[z] = bins_f[z] + lax.select(hit, tf_row, none)
                 bins_c[z] = bins_c[z] + lax.select(hit, tc_row, none)
@@ -351,10 +376,7 @@
         weight = weights[k] * DT
         x = xs.at[k]
         if k == 2:
-            for m in (2, 0, 1):
-                xflat = xs.at[m].reshape(42 * 8, 128)
-                for s in range(8):
-                    xflat[pl.ds(s, 42, stride=8), :] = states[m, :, s * 128 : (s + 1) * 128].astype(F32)
+            unpack_state(2)
         squares = []
         for n in range(3):
             squares.append(sum(x[c * 3 + n] * x[c * 3 + n] for c in range(4)))
@@ -380,14 +402,25 @@
                 copy.start()
 
         last = ZCOMP if k == 2 else QCOMP
-        halves = from_diag(tab, 0, 2)
-        for h in range(2):
-            for j in range(2):
-                sdiag[k, j, h * 8 : h * 8 + 8] = halves[h][j] * d_scale[h]
+        if k < 2:
+            pack_diag(k, from_diag(tab, 0, 2), d_scale)
+        slot_scale = lambda c: slot_edge if c < 4 else slot_kedge
+        fill_slots(k, tab, list(range(COMPS, last + 1)) + list(range(SPLIT)), 2, slot_scale)
         if k == 2:
+            halves = from_diag(tab, 0, 2)
             pl.semaphore_wait(barrier, greeters)
-        send(diag_copy, k, DIAG, (0, 1, 2, 3))
-        send_slots(k, tab, range(last + 1), 0, lambda c: slot_edge if c < 4 else slot_kedge)
+            pack_diag(k, halves, d_scale)
+        send(first_copy, k, MAIN, (0, 3, 1, 2))
+        fill_slots(k, tab, range(SPLIT, COMPS), 2, slot_scale)
+        send(second_copy, k, MAIN, (0, 3, 1, 2))
+
+        if k == 2:
+            for m in (0, 1):
+                unpack_state(m)
+            for small, wide, size in ((vol_ref, vol, 12), (fin_ref, fin, 8), (fout_ref, fout, 8)):
+                for b in range(size):
+                    for a in range(size):
+                        wide[b * size + a] = jnp.broadcast_to(small[b : b + 1, a : a + 1], TILE)
 
         if k == 2:
             for f in range(3):
@@ -399,10 +432,10 @@
                 pair = from_partner(tab, c, f)
                 if c < COMPS:
                     scale = kept[f] if c < 4 else kept[3 + f]
-                    local[f, c * 2] = pair[0] * scale
-                    local[f, c * 2 + 1] = pair[1] * scale
+                    local[f, c * 2 + 2] = pair[0] * scale
+                    local[f, c * 2 + 3] = pair[1] * scale
                 else:
-                    local[f, 28 + c - COMPS] = pair[0]
+                    local[f, c - COMPS] = pair[0]
 
         if k > 0:
             tf, tc, wet_friction = own_terms(k, v, x, weight, tf, tc)
@@ -432,18 +465,16 @@
 
         if k == 2:
             halves = from_diag(xs.at[0], 4, 1) + from_diag(xs.at[0], 6, 1)
-            for h in range(2):
-                for j in range(2):
-                    sdiag[FWD, j, h * 8 : h * 8 + 8] = halves[h][j]
-            send(diag_copy, FWD, DIAG, (0, 1, 2, 3))
-            send_slots(FWD, xs.at[0], range(4, COMPS), 8, None)
+            pack_diag(FWD, halves, None)
+            fill_slots(FWD, xs.at[0], range(4, COMPS), -8, None)
+            send(forward_copy, FWD, MAIN, (0, 3, 1, 2))
         if k == 1:
             for f in range(3):
                 for c in range(4, COMPS):
                     pair = from_partner(xs.at[0], c, f)
                     fwd[f, c * 2 - 8] = pair[0]
                     fwd[f, c * 2 - 7] = pair[1]
-            arrive(main_copy, FWD, MAIN, range(4))
+            arrive(forward_copy, FWD, MAIN, range(4))
             arrive(diag_copy, FWD, DIAG, range(4))
             merge_diag(FWD)
             receive(FWD, fwd, range(20), range(8))
@@ -461,33 +492,44 @@
             for copy in gx_copies:
                 copy.start()
 
-        channels = range(30 if k == 2 else 29)
-        arrive(main_copy, k, MAIN, (1, 2))
-        receive(k, local, channels, range(2, 6))
-        arrive(main_copy, k, MAIN, (0, 3))
-        receive(k, local, channels, (0, 1, 6, 7))
+        early = [ch for ch in range(FIRST) if ch != 1 or k == 2]
+        late = range(FIRST, 30)
+        terms = [jnp.zeros(TILE, F32)] * 3
+
+        def porewater(f, channels):
+            for ch in channels:
+                r = 12 + ((ch - 10) // 2) * 3 + FACE_NODES[f][ch % 2]
+                value = receive_diag(k, local, f, ch, ch // 2 - 1, ch % 2)
+                if k > 0:
+                    terms[f] = terms[f] + value * x[r]
+                pre[r] = pre[r] + value
+
+        arrive(first_copy, k, MAIN, (1, 2))
+        receive(k, local, early, range(2, 6))
+        arrive(second_copy, k, MAIN, (1, 2))
+        receive(k, local, late, range(2, 6))
+        arrive(first_copy, k, MAIN, (0, 3))
+        receive(k, local, early, (0, 1, 6, 7))
         arrive(diag_copy, k, DIAG, range(4))
         merge_diag(k)
         for f in range(3):
             if k == 2:
-                kept[6 + f] = receive_diag(k, local, f, 29, ZCOMP, 0)
-            outer_q = receive_diag(k, local, f, 28, QCOMP, 0)
+                kept[6 + f] = receive_diag(k, local, f, 1, ZCOMP, 0)
+            outer_q = receive_diag(k, local, f, 0, QCOMP, 0)
             half_speed = 0.5 * jnp.sqrt(1.0 + 0.03125 * (q[f] + outer_q))
-            outer = [receive_diag(k, local, f, a, a // 2, a % 2) for a in range(8)]
+            outer = [receive_diag(k, local, f, a + 2, a // 2, a % 2) for a in range(8)]
             for a in range(8):
                 r = (a // 2) * 3 + FACE_NODES[f][a % 2]
                 total = half_speed * (edge[f] * tab[r] - outer[a])
                 for b in range(8):
                     total = total - fout[b * 8 + a] * outer[b]
                 pre[r] = pre[r] + total
-            term = jnp.zeros(TILE, F32)
-            for ch in range(8, 28):
-                r = 12 + ((ch - 8) // 2) * 3 + FACE_NODES[f][ch % 2]
-                value = receive_diag(k, local, f, ch, ch // 2, ch % 2)
-                if k > 0:
-                    term = term + value * x[r]
-                pre[r] = pre[r] + value
-            far_terms[f] = far_terms[f] + weight * term
+            porewater(f, range(10, FIRST))
+        arrive(second_copy, k, MAIN, (0, 3))
+        receive(k, local, late, (0, 1, 6, 7))
+        for f in range(3):
+            porewater(f, late)
+            far_terms[f] = far_terms[f] + weight * terms[f]
 
         for r in range(42):
             if k == 2:
@@ -520,6 +562,23 @@
     zone_conductivity, wet_mask, element_zone, send_face, send_count, face_partner, volume_matrix, flux_in, flux_out,
 ):
     vmem = pl.BlockSpec(memory_space=pltpu.VMEM)
+    arrays = (
+        cotangent.reshape(42, 8, 128),
+        section_states.reshape(3, 42, 1024),
+        inverse_area.reshape(8, 128),
+        edge_length.reshape(3, 8, 128),
+        roughness.reshape(8, 128),
+        soil_conductance.reshape(8, 128),
+        zone_friction.reshape(4, 128),
+        zone_conductivity.reshape(4, 128),
+        wet_mask.reshape(8, 128),
+        element_zone.reshape(8, 128),
+        send_face.reshape(8, 256),
+        face_partner.reshape(3, 8, 128),
+        volume_matrix,
+        flux_in,
+        flux_out,
+    )
     adjoint, grads = pl.pallas_call(
         kernel,
         out_shape=(
@@ -557,40 +616,24 @@
             pltpu.VMEM((9, 8, 128), F32),
             pltpu.VMEM((4, 4, 30, 2, 128), F32),
             pltpu.VMEM((4, 4, 30, 2, 128), F32),
-            pltpu.VMEM((4, 2, 16, 128), F32),
-            pltpu.VMEM((4, 4, 2, 16, 128), F32),
+            pltpu.VMEM((4, 8, 128), F32),
+            pltpu.VMEM((4, 4, 8, 128), F32),
             pltpu.VMEM((4, 2, 16, 128), F32),
             pltpu.VMEM((GY, 8, 128), F32),
             pltpu.VMEM((GX, 8, 128), F32),
             pltpu.SemaphoreType.DMA((15,)),
-            pltpu.SemaphoreType.DMA((4, 8)),
-            pltpu.SemaphoreType.DMA((4, 8)),
+            pltpu.SemaphoreType.DMA((4, 12)),
+            pltpu.SemaphoreType.DMA((4, 12)),
             pltpu.SemaphoreType.DMA((GY,)),
             pltpu.SemaphoreType.DMA((GY,)),
             pltpu.SemaphoreType.DMA((GX,)),
             pltpu.SemaphoreType.DMA((GX,)),
         ],
         compiler_params=pltpu.CompilerParams(
-            collective_id=0, has_side_effects=True, vmem_limit_bytes=63 << 20
+            collective_id=0, has_side_effects=True, vmem_limit_bytes=32 << 20
         ),
         name="sections",
-    )(
-        cotangent.reshape(42, 8, 128),
-        section_states.reshape(3, 42, 1024),
-        inverse_area.reshape(8, 128),
-        edge_length.reshape(3, 8, 128),
-        roughness.reshape(8, 128),
-        soil_conductance.reshape(8, 128),
-        zone_friction.reshape(4, 128),
-        zone_conductivity.reshape(4, 128),
-        wet_mask.reshape(8, 128),
-        element_zone.reshape(8, 128),
-        send_face.reshape(8, 256),
-        face_partner.reshape(3, 8, 128),
-        volume_matrix,
-        flux_in,
-        flux_out,
-    )
+    )(*[pltpu.with_memory_space_constraint(array, pltpu.MemorySpace.HBM) for array in arrays])
     return adjoint.reshape(1, 1, 42, 1024), grads
 
 

time: 31.6 us -> 29.6 us (0.937)
  Pallas kernels: 28.6 us -> 27.6 us
  local copies, waits for them, and re-layouts: 2.2 us -> 1.26 us
    pallas_call x1, Pallas kernels: 28.6 us -> 27.6 us  [local(): pl.pallas_call(kernel, out_shape=(jax.ShapeDtypeStruct((42, 8, 128), F32)...]
    unnamed x4 -> x2, local copies, waits for them, and re-layouts: 2.2 us -> 1.26 us
where the time goes in v3:
time: 29.6 us; the launch traced here: 29.5 us
  Pallas kernels  27.6 us (93%)
  local copies, waits for them, and re-layouts  1.26 us (4%)
  between operations  0.64 us (2%)
    pallas_call x1, Pallas kernels, local(): pl.pallas_call(kernel, out_shape=(jax.ShapeDtypeStruct((42, 8, 128), F32)...  27.6 us
    unnamed x2, local copies, waits for them, and re-layouts  1.26 us

profile of v3, /device:TPU:1, one launch (start us, length us, event | category | flops | bytes accessed | tf_op | source)
XLA Modules:
  0.0 29.5 jit_solution(11711540494667890041)
XLA Ops:
  0.6 27.6 %sections.1 = (f32[42,8,128]{2,1,0:T(8,128)S(1)}, f32[2,512]{1,0:T(2,128)S(1)}) custom-call(f32[42,8,128]{2,1,0:T(8,128)} %bitcast.15, bf16[3,42,1024]{2,1,0:T(8,128)(2,1)} %bitcast.14, f32[8,128]{1,0:T(8,128)} %bitcast.19, f32[3,8,128]{2,1,0:T(8,128)} %bitcast.16, f32[8,128]{1,0:T(8,128)} %bitcast.20, f32[8,128]{1,0:T(8,128)} %bitcast.21, ...), custom_call_target="tpu_custom_call" | custom-call | tf_op jit(solution)/shard_map/sections/pallas_call | solution.py:582
  28.2 0.7 %copy.21 = f32[1,1,42,1024]{3,1,2,0:T(1,128)} copy(f32[1,1,42,1024]{3,1,2,0:T(1,128)S(1)} %bitcast.13) | data formatting | bytes 344064
  28.9 0.6 %copy.22 = f32[2,512]{1,0:T(2,128)} copy(f32[2,512]{1,0:T(2,128)S(1)} %get-tuple-element.13) | data formatting | bytes 8192

commit v4 on v3

--- a/solution.py
+++ b/solution.py
@@ -321,7 +321,7 @@
         return tf, tc, wet * rough_zone * moment
 
     def zone_bins(tf, tc):
-        bins_f = [jnp.zeros(TILE, F32) for _ in range(WINDOW // 8)]
+        bins_f = jnp.zeros(TILE, F32)
         bins_c = [jnp.zeros(TILE, F32) for _ in range(WINDOW // 8)]
         none = jnp.zeros(TILE, F32)
         own_rel = relative(zone)
@@ -330,31 +330,24 @@
             rel = jnp.broadcast_to(own_rel[s : s + 1], TILE) - sub
             tf_row = jnp.broadcast_to(tf[s : s + 1], TILE)
             tc_row = jnp.broadcast_to(tc[s : s + 1], TILE)
-            for z in (5,):
-                hit = rel == 8 * z
-                bins_f[z] = bins_f[z] + lax.select(hit, tf_row, none)
-                bins_c[z] = bins_c[z] + lax.select(hit, tc_row, none)
+            hit = rel == BEHIND
+            bins_f = bins_f + lax.select(hit, tf_row, none)
+            bins_c[BEHIND // 8] = bins_c[BEHIND // 8] + lax.select(hit, tc_row, none)
             for f in range(3):
                 rel = jnp.broadcast_to(far_rel[f][s : s + 1], TILE) - sub
                 term = jnp.broadcast_to(far_terms[f][s : s + 1], TILE)
-                for z in range(WINDOW // 8):
+                for z in (0, 1, 2, 4, 5, 6, 8, 9, 10):
                     bins_c[z] = bins_c[z] + lax.select(rel == 8 * z, term, none)
-        ones = jnp.ones(TILE, F32)
-        pad = [jnp.zeros(TILE, F32) for _ in range(16 - WINDOW // 8)]
-
-        def lanes(bins):
-            return lax.dot_general(
-                ones, jnp.concatenate(bins + pad, axis=0), (((1,), (1,)), ((), ())),
-                precision=lax.Precision.HIGHEST, preferred_element_type=F32,
-            )
-
-        friction_row, conduct_row = lanes(bins_f), lanes(bins_c)
+        rows = jnp.concatenate(bins_c + [bins_f] + [none] * (15 - WINDOW // 8), axis=0)
+        sums = lax.dot_general(
+            jnp.ones(TILE, F32), rows, (((1,), (1,)), ((), ())),
+            precision=lax.Precision.HIGHEST, preferred_element_type=F32,
+        )
         rel = relative((sub >> 1) * 128 + lane)
-        at_rel = lanes_of(rel & 127)
-        spread = jnp.where(
-            (sub & 1) == 0, take(friction_row, at_rel), take(conduct_row, at_rel)
-        )
-        return jnp.where(rel < WINDOW, spread, 0.0)
+        is_friction = (sub & 1) == 0
+        own_zone = (rel >= BEHIND) & (rel < BEHIND + 8)
+        found = take(sums, lanes_of(jnp.where(is_friction, rel + (WINDOW - BEHIND), rel) & 127))
+        return jnp.where(is_friction, jnp.where(own_zone, found, 0.0), jnp.where(rel < WINDOW, found, 0.0))
 
     gy_copies = [
         pltpu.make_async_remote_copy(
@@ -468,12 +461,12 @@
             pack_diag(FWD, halves, None)
             fill_slots(FWD, xs.at[0], range(4, COMPS), -8, None)
             send(forward_copy, FWD, MAIN, (0, 3, 1, 2))
-        if k == 1:
             for f in range(3):
                 for c in range(4, COMPS):
                     pair = from_partner(xs.at[0], c, f)
                     fwd[f, c * 2 - 8] = pair[0]
                     fwd[f, c * 2 - 7] = pair[1]
+        if k == 1:
             arrive(forward_copy, FWD, MAIN, range(4))
             arrive(diag_copy, FWD, DIAG, range(4))
             merge_diag(FWD)
@@ -555,6 +548,15 @@
             make(k, i).wait_send()
     for copy in gy_copies + gx_copies:
         copy.wait_send()
+
+
+def deliver(adjoint, grads, adjoint_out, grads_out, sem):
+    first = pltpu.make_async_copy(adjoint, adjoint_out, sem.at[0])
+    second = pltpu.make_async_copy(grads, grads_out, sem.at[1])
+    first.start()
+    second.start()
+    first.wait()
+    second.wait()
 
 
 def local(
@@ -634,6 +636,17 @@
         ),
         name="sections",
     )(*[pltpu.with_memory_space_constraint(array, pltpu.MemorySpace.HBM) for array in arrays])
+    adjoint, grads = pl.pallas_call(
+        deliver,
+        out_shape=(
+            jax.ShapeDtypeStruct((42, 8, 128), F32),
+            jax.ShapeDtypeStruct((2, ZONES), F32),
+        ),
+        in_specs=[vmem, vmem],
+        out_specs=(pl.BlockSpec(memory_space=pltpu.MemorySpace.HBM),) * 2,
+        scratch_shapes=[pltpu.SemaphoreType.DMA((2,))],
+        name="deliver",
+    )(*[pltpu.with_memory_space_constraint(array, pltpu.MemorySpace.VMEM) for array in (adjoint, grads)])
     return adjoint.reshape(1, 1, 42, 1024), grads
 
 

time: 29.6 us -> 29.1 us (0.983)
  local copies, waits for them, and re-layouts: 1.26 us -> 0 us
  Pallas kernels: 27.6 us -> 28.3 us
    unnamed x2 -> x0, local copies, waits for them, and re-layouts: 1.26 us -> none
    pallas_call x0 -> x1, Pallas kernels: none -> 0.69 us  [local(): pl.pallas_call(deliver, out_shape=(jax.ShapeDtypeStruct((42, 8, 128), F32...]
where the time goes in v4:
time: 29.1 us; the launch traced here: 28.9 us
  Pallas kernels  28.3 us (97%)
  between operations  0.64 us (2%)
    pallas_call x1, Pallas kernels, local(): pl.pallas_call(kernel, out_shape=(jax.ShapeDtypeStruct((42, 8, 128), F32)...  27.6 us
    pallas_call x1, Pallas kernels, local(): pl.pallas_call(deliver, out_shape=(jax.ShapeDtypeStruct((42, 8, 128), F32...  0.69 us

profile of v4, /device:TPU:1, one launch (start us, length us, event | category | flops | bytes accessed | tf_op | source)
XLA Modules:
  0.0 28.9 jit_solution(393350965131119410)
XLA Ops:
  0.6 27.6 %sections.1 = (f32[42,8,128]{2,1,0:T(8,128)S(1)}, f32[2,512]{1,0:T(2,128)S(1)}) custom-call(f32[42,8,128]{2,1,0:T(8,128)} %bitcast.14, bf16[3,42,1024]{2,1,0:T(8,128)(2,1)} %bitcast.13, f32[8,128]{1,0:T(8,128)} %bitcast.18, f32[3,8,128]{2,1,0:T(8,128)} %bitcast.15, f32[8,128]{1,0:T(8,128)} %bitcast.19, f32[8,128]{1,0:T(8,128)} %bitcast.20, ...), custom_call_target="tpu_custom_call" | custom-call | tf_op jit(solution)/shard_map/sections/pallas_call | solution.py:584
  28.2 0.7 %deliver.1 = (f32[42,8,128]{2,1,0:T(8,128)}, f32[2,512]{1,0:T(2,128)}) custom-call(f32[42,8,128]{2,1,0:T(8,128)S(1)} %get-tuple-element.6.adjoint, f32[2,512]{1,0:T(2,128)S(1)} %get-tuple-element.7.grads), custom_call_target="tpu_custom_call" | custom-call | tf_op jit(solution)/shard_map/deliver/pallas_call | solution.py:639

commit v5 on v4

--- a/solution.py
+++ b/solution.py
@@ -343,8 +343,8 @@
             jnp.ones(TILE, F32), rows, (((1,), (1,)), ((), ())),
             precision=lax.Precision.HIGHEST, preferred_element_type=F32,
         )
-        rel = relative((sub >> 1) * 128 + lane)
-        is_friction = (sub & 1) == 0
+        rel = (lane - base + (BEHIND + ZONES)) & 127
+        is_friction = sub == 0
         own_zone = (rel >= BEHIND) & (rel < BEHIND + 8)
         found = take(sums, lanes_of(jnp.where(is_friction, rel + (WINDOW - BEHIND), rel) & 127))
         return jnp.where(is_friction, jnp.where(own_zone, found, 0.0), jnp.where(rel < WINDOW, found, 0.0))
@@ -390,7 +390,7 @@
                     r = 12 + ((ch - 8) // 2) * 3 + FACE_NODES[f][ch % 2]
                     term = term + fwd[f, ch - 8] * tab[r]
                 tc = tc + weight * kedge[f] * term
-            gyb[iy] = zone_bins(tf, tc)
+            gyb[iy] = zone_bins(tf, tc)[0:2]
             for copy in gy_copies:
                 copy.start()
 
@@ -534,14 +534,18 @@
 
     for copy in gx_copies:
         copy.wait_recv()
-    total = gxb[0]
-    for i in range(1, GX):
-        total = total + gxb[i]
+    lane2 = lax.broadcasted_iota(jnp.int32, (2, 128), 1)
+    blocks = [jnp.zeros((2, 128), F32) for _ in range(4)]
+    for i in range(GX):
+        start = (4 * GY * i - BEHIND) % ZONES
+        block, lane_at = start // 128, start % 128
+        value = gxb[i]
+        blocks[block] = blocks[block] + jnp.where(lane2 >= lane_at, value, 0.0)
+        after = (block + 1) % 4
+        blocks[after] = blocks[after] + jnp.where(lane2 >= lane_at, 0.0, value)
     for t in range(4):
-        grads[0:1, t * 128 : (t + 1) * 128] = GRAD_WEIGHT * total[2 * t : 2 * t + 1]
-        grads[1:2, t * 128 : (t + 1) * 128] = (
-            GRAD_WEIGHT * total[2 * t + 1 : 2 * t + 2] / zc_ref[t : t + 1]
-        )
+        grads[0:1, t * 128 : (t + 1) * 128] = GRAD_WEIGHT * blocks[t][0:1]
+        grads[1:2, t * 128 : (t + 1) * 128] = GRAD_WEIGHT * blocks[t][1:2] / zc_ref[t : t + 1]
     for make, k, table, i in sends:
         @pl.when(exists(table[i]))
         def _():
@@ -621,8 +625,8 @@
             pltpu.VMEM((4, 8, 128), F32),
             pltpu.VMEM((4, 4, 8, 128), F32),
             pltpu.VMEM((4, 2, 16, 128), F32),
-            pltpu.VMEM((GY, 8, 128), F32),
-            pltpu.VMEM((GX, 8, 128), F32),
+            pltpu.VMEM((GY, 2, 128), F32),
+            pltpu.VMEM((GX, 2, 128), F32),
             pltpu.SemaphoreType.DMA((15,)),
             pltpu.SemaphoreType.DMA((4, 12)),
             pltpu.SemaphoreType.DMA((4, 12)),

time: 29.1 us -> 28.9 us (level)
  no operation moved by 1% of the time
where the time goes in v5:
time: 28.9 us; the launch traced here: 28.8 us
  Pallas kernels  28.2 us (98%)
  between operations  0.64 us (2%)
    pallas_call x1, Pallas kernels, local(): pl.pallas_call(kernel, out_shape=(jax.ShapeDtypeStruct((42, 8, 128), F32)...  27.5 us
    pallas_call x1, Pallas kernels, local(): pl.pallas_call(deliver, out_shape=(jax.ShapeDtypeStruct((42, 8, 128), F32...  0.69 us

profile of v5, /device:TPU:1, one launch (start us, length us, event | category | flops | bytes accessed | tf_op | source)
XLA Modules:
  0.0 28.8 jit_solution(7087830897635103659)
XLA Ops:
  0.6 27.5 %sections.1 = (f32[42,8,128]{2,1,0:T(8,128)S(1)}, f32[2,512]{1,0:T(2,128)S(1)}) custom-call(f32[42,8,128]{2,1,0:T(8,128)} %bitcast.14, bf16[3,42,1024]{2,1,0:T(8,128)(2,1)} %bitcast.13, f32[8,128]{1,0:T(8,128)} %bitcast.18, f32[3,8,128]{2,1,0:T(8,128)} %bitcast.15, f32[8,128]{1,0:T(8,128)} %bitcast.19, f32[8,128]{1,0:T(8,128)} %bitcast.20, ...), custom_call_target="tpu_custom_call" | custom-call | tf_op jit(solution)/shard_map/sections/pallas_call | solution.py:588
  28.1 0.7 %deliver.1 = (f32[42,8,128]{2,1,0:T(8,128)}, f32[2,512]{1,0:T(2,128)}) custom-call(f32[42,8,128]{2,1,0:T(8,128)S(1)} %get-tuple-element.6.adjoint, f32[2,512]{1,0:T(2,128)S(1)} %get-tuple-element.7.grads), custom_call_target="tpu_custom_call" | custom-call | tf_op jit(solution)/shard_map/deliver/pallas_call | solution.py:643

commit v6 on v5

--- a/solution.py
+++ b/solution.py
@@ -614,7 +614,7 @@
             pltpu.VMEM((64, 8, 128), F32),
             pltpu.VMEM((48, 8, 128), F32),
             pltpu.VMEM((24, 8, 128), F32),
-            pltpu.VMEM((3, 42, 8, 128), F32),
+            pltpu.VMEM((4, 42, 8, 128), F32),
             pltpu.VMEM((3, 30, 8, 128), F32),
             pltpu.VMEM((3, 20, 8, 128), F32),
             pltpu.VMEM((42, 8, 128), F32),

time: 28.9 us -> 28.9 us (level)
  no operation moved by 1% of the time
where the time goes in v6:
time: 28.9 us; the launch traced here: 28.8 us
  Pallas kernels  28.2 us (98%)
  between operations  0.64 us (2%)
    pallas_call x1, Pallas kernels, local(): pl.pallas_call(kernel, out_shape=(jax.ShapeDtypeStruct((42, 8, 128), F32)...  27.5 us
    pallas_call x1, Pallas kernels, local(): pl.pallas_call(deliver, out_shape=(jax.ShapeDtypeStruct((42, 8, 128), F32...  0.69 us

profile of v6, /device:TPU:1, one launch (start us, length us, event | category | flops | bytes accessed | tf_op | source)
XLA Modules:
  0.0 28.8 jit_solution(17489433495097092956)
XLA Ops:
  0.6 27.5 %sections.1 = (f32[42,8,128]{2,1,0:T(8,128)S(1)}, f32[2,512]{1,0:T(2,128)S(1)}) custom-call(f32[42,8,128]{2,1,0:T(8,128)} %bitcast.14, bf16[3,42,1024]{2,1,0:T(8,128)(2,1)} %bitcast.13, f32[8,128]{1,0:T(8,128)} %bitcast.18, f32[3,8,128]{2,1,0:T(8,128)} %bitcast.15, f32[8,128]{1,0:T(8,128)} %bitcast.19, f32[8,128]{1,0:T(8,128)} %bitcast.20, ...), custom_call_target="tpu_custom_call" | custom-call | tf_op jit(solution)/shard_map/sections/pallas_call | solution.py:588
  28.1 0.7 %deliver.1 = (f32[42,8,128]{2,1,0:T(8,128)}, f32[2,512]{1,0:T(2,128)}) custom-call(f32[42,8,128]{2,1,0:T(8,128)S(1)} %get-tuple-element.6.adjoint, f32[2,512]{1,0:T(2,128)S(1)} %get-tuple-element.7.grads), custom_call_target="tpu_custom_call" | custom-call | tf_op jit(solution)/shard_map/deliver/pallas_call | solution.py:643
